TPU v7x, 32 devices: a whole 2x2x4 slice. The times are simulated.
32 devices in a mesh: basin: 2 (over y), row: 4 (over z), col: 2 (over x), sub: 2 (over core).
Axes of the slice: x: 2, y: 2, z: 4, core: 2. Of those that a mesh axis runs over, the one named last changes fastest.
Arguments:
- water_depth: float32 [256, 128, 128], P(('basin', 'row', 'col', 'sub')), parts along dimension 0, may hold values from 0.1 to 3
- flow_east: float32 [256, 128, 128], P(('basin', 'row', 'col', 'sub')), parts along dimension 0, may hold values from -3 to 3
- flow_south: float32 [256, 128, 128], P(('basin', 'row', 'col', 'sub')), parts along dimension 0, may hold values from -3 to 3
- bed_level: float32 [256, 128, 128], P(('basin', 'row', 'col', 'sub')), parts along dimension 0, may hold values from -2 to 2
- manning_n: float32 [256, 128, 128], P(('basin', 'row', 'col', 'sub')), parts along dimension 0, may hold values from 0.03 to 0.15
- placed_before: int32 [256], P('basin'), parts along dimension 0, may hold values from 0 to 127, as said below
- placed_after: int32 [256], P('basin'), parts along dimension 0, may hold values from 0 to 127, as said below
- wet_tiles: int32 [256], P('basin'), parts along dimension 0, may hold values 0 or 1
Outputs:
- new_depth: float32 [256, 128, 128], P(('basin', 'row', 'col', 'sub')), parts along dimension 0
- new_flow_east: float32 [256, 128, 128], P(('basin', 'row', 'col', 'sub')), parts along dimension 0
- new_flow_south: float32 [256, 128, 128], P(('basin', 'row', 'col', 'sub')), parts along dimension 0
There are 2 independent parts, one for each index of `basin`. A program takes and returns all parts, laid end to end along the dimension named above; each array names one. Nothing has to cross between parts.
Inputs may be any that keep to these rules, and one draw needn't show every extreme that they name: placed_before holds every tile once. Slot s lies on the device of index s // 8 over row, col and sub together; the tiles of tile row r sit on the devices of row index r. placed_after holds every tile once. A tile either keeps its slot of placed_before or goes to a slot on another device of the same row index. Each device gives up exactly 4 tiles and takes exactly 4, at most 2 of them from any one device.
All inputs are finite; a program needn't handle non-finite values.
Results may differ from a plain program's by a relative error of at most 0.00002.
Values sent between devices are 32-bit elements; how exact they have to be, the bound alone decides.
A program may use at most 64 MiB of HBM per device.

v0:
```python
import jax
import jax.numpy as jnp
from jax import lax
from jax.sharding import PartitionSpec as P

STEPS = 6
FIRST = 3


GRAV = 9.81
STEP_TIME = 0.5
SPACING = 5.0
RATE = 0.1
DEPTH_FLOOR = 0.3


def padded(array, sides, width):
    for axis, dim in sides:
        size, length = (lax.axis_size(axis), array.shape[dim])
        up = [(i, (i + 1) % size) for i in range(size - 1)]
        down = [(j, i) for i, j in up]
        last = lax.slice_in_dim(array, length - width, length, axis=dim)
        first = lax.slice_in_dim(array, 0, width, axis=dim)
        before = lax.ppermute(last, axis, up)
        after = lax.ppermute(first, axis, down)
        array = jnp.concatenate([before, array, after], axis=dim)
    return array


def face_flow(discharge, surface, surface_next, ground, ground_next, manning):
    wetted = jnp.maximum(surface, surface_next) - jnp.maximum(ground, ground_next)
    pressure = GRAV * STEP_TIME * jnp.maximum(wetted, 0.0) * (surface_next - surface) / SPACING
    resistance = 1.0 + GRAV * STEP_TIME * manning * manning * jnp.abs(discharge) / jnp.power(
        jnp.maximum(wetted, DEPTH_FLOOR), 7.0 / 3.0
    )
    return (discharge - pressure) / resistance


def inverse(ordering):
    entries = ordering.shape[0]
    return jnp.zeros((entries,), jnp.int32).at[ordering].set(jnp.arange(entries, dtype=jnp.int32))


def shards(
    water_depth, flow_east, flow_south, bed_level, manning_n, placed_before, placed_after, wet_tiles
):
    tile_count = water_depth.shape[0]
    tile_side = water_depth.shape[1]
    lane_count = lax.axis_size(("col", "sub"))
    row_tiles = lane_count * tile_count
    slot_total = placed_before.shape[0]
    device_total = slot_total // tile_count
    row_total = slot_total // row_tiles
    my_row = lax.axis_index("row")
    my_device = my_row * lane_count + lax.axis_index(("col", "sub"))
    my_slots = my_device * tile_count + jnp.arange(tile_count, dtype=jnp.int32)
    where_before = inverse(placed_before)
    where_after = inverse(placed_after)
    wet_flags = wet_tiles == 1
    columns = jnp.arange(tile_side, dtype=jnp.int32)
    slot_ids = jnp.arange(tile_count, dtype=jnp.int32)

    def near_index(slot_list):
        return (slot_list // row_tiles - my_row + 1) * row_tiles + slot_list % row_tiles

    def share_edges(edge_rows):
        row_group = lax.all_gather(edge_rows[None], ("col", "sub"), axis=1, tiled=True)
        spread = padded(row_group, (("row", 0),), 1)
        return spread.reshape(3 * row_tiles, 2, tile_side)

    def tile_links(tile_ids, where_now):
        column = tile_ids % row_tiles
        tile_row = tile_ids // row_tiles
        has_east = column < row_tiles - 1
        has_west = column > 0
        has_south = tile_row < row_total - 1
        has_north = tile_row > 0
        east_tile = jnp.where(has_east, tile_ids + 1, tile_ids)
        west_tile = jnp.where(has_west, tile_ids - 1, tile_ids)
        south_tile = jnp.where(has_south, tile_ids + row_tiles, tile_ids)
        north_tile = jnp.where(has_north, tile_ids - row_tiles, tile_ids)
        mine_wet = wet_flags[tile_ids]
        return (
            mine_wet,
            mine_wet & has_east & wet_flags[east_tile],
            mine_wet & has_south & wet_flags[south_tile],
            mine_wet & has_west & wet_flags[west_tile],
            mine_wet & has_north & wet_flags[north_tile],
            near_index(where_now[east_tile]),
            near_index(where_now[south_tile]),
            near_index(where_now[west_tile]),
            near_index(where_now[north_tile]),
            near_index(where_before[east_tile]),
            near_index(where_before[south_tile]),
        )

    bed_near = share_edges(jnp.stack([bed_level[:, :, 0], bed_level[:, 0, :]], axis=1))
    layout = tile_links(placed_before[my_slots], where_before)
    fields = (water_depth, flow_east, flow_south, bed_level, manning_n)
    for step_index in range(STEPS):
        if step_index == FIRST:
            field_count = len(fields)
            stacked = jnp.stack(fields, axis=1)
            dest_device = where_after[placed_before] // tile_count
            home_device = jnp.arange(slot_total, dtype=jnp.int32) // tile_count
            grid_leave = (dest_device != home_device).reshape(device_total, tile_count)
            earlier = slot_ids[None, :] < slot_ids[:, None]
            source = where_before[placed_after[my_slots]]
            source_device = source // tile_count
            staying = source_device == my_device
            source_lane = source_device % lane_count
            kept_tiles = stacked[source % tile_count]
            mine_leave = grid_leave[my_device]
            move_out = min(tile_count // 2, 2 * (lane_count - 1))
            rank_out = jnp.sum((grid_leave[:, None, :] & earlier[None]).astype(jnp.int32), axis=2)
            mine_rank = rank_out[my_device]
            wanted = mine_leave[None, :] & (
                mine_rank[None, :] == jnp.arange(move_out, dtype=jnp.int32)[:, None]
            )
            chosen_slots = jnp.sum(jnp.where(wanted, slot_ids[None, :], 0), axis=1)
            position = source_lane * move_out + rank_out.reshape(-1)[source]
            block_piece = lax.all_gather(stacked[chosen_slots], ("col", "sub"), axis=0, tiled=True)
            piece_rows = block_piece.shape[0]
            inside = (position >= 0) & (position < piece_rows) & jnp.logical_not(staying)
            chosen = block_piece[jnp.clip(position, 0, piece_rows - 1)]
            arrived = jnp.where(inside[:, None, None, None], chosen, jnp.zeros_like(stacked))
            placed = jnp.where(staying[:, None, None, None], kept_tiles, arrived)
            fields = tuple((placed[:, field_index] for field_index in range(field_count)))
            layout = tile_links(placed_after[my_slots], where_after)
        depth_now, flow_x, flow_y, ground, manning = fields
        (
            advance_mine_wet,
            open_east,
            open_south,
            open_west,
            open_north,
            east_now,
            south_now,
            west_now,
            north_now,
            east_bed,
            south_bed,
        ) = layout
        edge_set = share_edges(jnp.stack([depth_now[:, :, 0], depth_now[:, 0, :]], axis=1))
        east_ground = bed_near[east_bed, 0]
        south_ground = bed_near[south_bed, 1]
        surface = depth_now + ground
        surface_east = jnp.concatenate(
            [surface[:, :, 1:], (edge_set[east_now, 0] + east_ground)[:, :, None]], axis=2
        )
        ground_east = jnp.concatenate([ground[:, :, 1:], east_ground[:, :, None]], axis=2)
        surface_south = jnp.concatenate(
            [surface[:, 1:, :], (edge_set[south_now, 1] + south_ground)[:, None, :]], axis=1
        )
        ground_south = jnp.concatenate([ground[:, 1:, :], south_ground[:, None, :]], axis=1)
        wet_cells = advance_mine_wet[:, None, None]
        interior = columns < tile_side - 1
        open_x = wet_cells & (interior[None, None, :] | open_east[:, None, None])
        open_y = wet_cells & (interior[None, :, None] | open_south[:, None, None])
        updated_x = face_flow(flow_x, surface, surface_east, ground, ground_east, manning)
        updated_y = face_flow(flow_y, surface, surface_south, ground, ground_south, manning)
        flow_x = jnp.where(wet_cells, jnp.where(open_x, updated_x, 0.0), flow_x)
        flow_y = jnp.where(wet_cells, jnp.where(open_y, updated_y, 0.0), flow_y)
        edge_flow = share_edges(
            jnp.stack([flow_x[:, :, tile_side - 1], flow_y[:, tile_side - 1, :]], axis=1)
        )
        west_in = jnp.where(open_west[:, None], edge_flow[west_now, 0], 0.0)
        north_in = jnp.where(open_north[:, None], edge_flow[north_now, 1], 0.0)
        inflow_x = jnp.concatenate([west_in[:, :, None], flow_x[:, :, :-1]], axis=2)
        inflow_y = jnp.concatenate([north_in[:, None, :], flow_y[:, :-1, :]], axis=1)
        depth_new = jnp.where(
            wet_cells, depth_now + RATE * (inflow_x - flow_x + inflow_y - flow_y), depth_now
        )
        depth_now, flow_x, flow_y = (depth_new, flow_x, flow_y)
        fields = (depth_now, flow_x, flow_y, fields[3], fields[4])
    return (fields[0], fields[1], fields[2])


def solution(mesh):
    placed = (
        P(("basin", "row", "col", "sub"), None, None),
        P(("basin", "row", "col", "sub"), None, None),
        P(("basin", "row", "col", "sub"), None, None),
        P(("basin", "row", "col", "sub"), None, None),
        P(("basin", "row", "col", "sub"), None, None),
        P("basin"),
        P("basin"),
        P("basin"),
    )
    return jax.shard_map(
        shards,
        mesh=mesh,
        in_specs=placed,
        out_specs=(
            P(("basin", "row", "col", "sub"), None, None),
            P(("basin", "row", "col", "sub"), None, None),
            P(("basin", "row", "col", "sub"), None, None),
        ),
        check_vma=False,
    )
```

profile of v0, /device:TPU:9, one launch (start us, length us, event | category | flops | bytes accessed | tf_op | source)
XLA Modules:
  0.0 333.0 jit_solution(3129552135304832213)
XLA Ops:
  9.2 5.7 %all-gather = f32[32,2,128]{2,1,0:T(2,128)S(1)} all-gather(f32[8,2,128]{2,1,0:T(2,128)S(1)} %copy.361), channel_id=2, replica_groups=mesh['basin'=2,'row'=4,'col'=2,'sub'=2] {'col','sub'}, dimensions={0}, use_global_device_ids=true | all-gather | bytes 40960 | tf_op jit(solution)/shard_map/all_gather | solution.py:67
  16.8 3.4 %collective-permute-start = (f32[1,32,2,128]{3,2,1,0:T(2,128)S(1)}, f32[1,32,2,128]{3,2,1,0:T(2,128)S(1)}, u32[]{:S(2)}, u32[]{:S(2)}) collective-permute-start(f32[1,32,2,128]{3,2,1,0:T(2,128)S(1)} %bitcast.554), channel_id=1, source_target_pairs={{0,4},{4,8},{8,12},{1,5},{5,9},{9,13},{2,6},{6,10},{10,14},{3,7},{... | collective-permute-start | bytes 98312 | tf_op jit(solution)/shard_map/ppermute | solution.py:24
  22.2 5.8 %all-gather.1 = f32[32,2,128]{2,1,0:T(2,128)S(1)} all-gather(f32[8,2,128]{2,1,0:T(2,128)S(1)} %copy.364), channel_id=3, replica_groups=mesh['basin'=2,'row'=4,'col'=2,'sub'=2] {'col','sub'}, dimensions={0}, use_global_device_ids=true | all-gather | bytes 40960 | tf_op jit(solution)/shard_map/all_gather | solution.py:67
  29.9 3.4 %collective-permute-start.2 = (f32[1,32,2,128]{3,2,1,0:T(2,128)S(1)}, f32[1,32,2,128]{3,2,1,0:T(2,128)S(1)}, u32[]{:S(2)}, u32[]{:S(2)}) collective-permute-start(f32[1,32,2,128]{3,2,1,0:T(2,128)S(1)} %bitcast.557), channel_id=1, source_target_pairs={{0,4},{4,8},{8,12},{1,5},{5,9},{9,13},{2,6},{6,10},{10,14},{3,7},{... | collective-permute-start | bytes 98312 | tf_op jit(solution)/shard_map/ppermute | solution.py:24
  57.6 3.6 %select_select_fusion.12 = (f32[8,128,128]{2,1,0:T(8,128)S(1)}, f32[8,128,128]{2,1,0:T(8,128)}, f32[8,128,128]{2,1,0:T(8,128)S(1)}, f32[8,128,128]{2,1,0:T(8,128)}) fusion(f32[8,128,128]{2,1,0:T(8,128)} %param.9, f32[8,128,128]{2,1,0:T(8,128)S(1)} %add.1217, f32[8,128,1]{2,1,0:T(8,128)} %copy.365, f32[8,128,127]{2,1,0:T(8,128)} %slice.356, ...), kind=kLoop, calls=%fused_computation.134 | loop fusion | flops 5242880 | bytes 6817800 | tf_op jit(solution)/shard_map/jit(_where)/select_n | solution.py:162
  61.6 5.8 %all-gather.2 = f32[32,2,128]{2,1,0:T(2,128)S(1)} all-gather(f32[8,2,128]{2,1,0:T(2,128)S(1)} %pad_maximum_fusion.27), channel_id=4, replica_groups=mesh['basin'=2,'row'=4,'col'=2,'sub'=2] {'col','sub'}, dimensions={0}, use_global_device_ids=true | all-gather | bytes 40960 | tf_op jit(solution)/shard_map/all_gather | solution.py:67
  69.3 3.4 %collective-permute-start.4 = (f32[1,32,2,128]{3,2,1,0:T(2,128)S(1)}, f32[1,32,2,128]{3,2,1,0:T(2,128)S(1)}, u32[]{:S(2)}, u32[]{:S(2)}) collective-permute-start(f32[1,32,2,128]{3,2,1,0:T(2,128)S(1)} %bitcast.560), channel_id=1, source_target_pairs={{0,4},{4,8},{8,12},{1,5},{5,9},{9,13},{2,6},{6,10},{10,14},{3,7},{... | collective-permute-start | bytes 98312 | tf_op jit(solution)/shard_map/ppermute | solution.py:24
  78.0 6.3 %all-gather.3 = f32[32,2,128]{2,1,0:T(2,128)S(1)} all-gather(f32[8,2,128]{2,1,0:T(2,128)S(1)} %pad_maximum_fusion.28), channel_id=5, replica_groups=mesh['basin'=2,'row'=4,'col'=2,'sub'=2] {'col','sub'}, dimensions={0}, use_global_device_ids=true | all-gather | bytes 40960 | tf_op jit(solution)/shard_map/all_gather | solution.py:67
  86.3 3.6 %collective-permute-start.6 = (f32[1,32,2,128]{3,2,1,0:T(2,128)S(1)}, f32[1,32,2,128]{3,2,1,0:T(2,128)S(1)}, u32[]{:S(2)}, u32[]{:S(2)}) collective-permute-start(f32[1,32,2,128]{3,2,1,0:T(2,128)S(1)} %bitcast.566), channel_id=1, source_target_pairs={{0,4},{4,8},{8,12},{1,5},{5,9},{9,13},{2,6},{6,10},{10,14},{3,7},{... | collective-permute-start | bytes 98312 | tf_op jit(solution)/shard_map/ppermute | solution.py:24
  94.2 3.1 select_select_fusion.10
  97.7 5.5 %all-gather.4 = f32[32,2,128]{2,1,0:T(2,128)S(1)} all-gather(f32[8,2,128]{2,1,0:T(2,128)S(1)} %pad_maximum_fusion.29), channel_id=6, replica_groups=mesh['basin'=2,'row'=4,'col'=2,'sub'=2] {'col','sub'}, dimensions={0}, use_global_device_ids=true | all-gather | bytes 40960 | tf_op jit(solution)/shard_map/all_gather | solution.py:67
  105.1 3.6 %collective-permute-start.8 = (f32[1,32,2,128]{3,2,1,0:T(2,128)S(1)}, f32[1,32,2,128]{3,2,1,0:T(2,128)S(1)}, u32[]{:S(2)}, u32[]{:S(2)}) collective-permute-start(f32[1,32,2,128]{3,2,1,0:T(2,128)S(1)} %bitcast.572), channel_id=1, source_target_pairs={{0,4},{4,8},{8,12},{1,5},{5,9},{9,13},{2,6},{6,10},{10,14},{3,7},{... | collective-permute-start | bytes 98312 | tf_op jit(solution)/shard_map/ppermute | solution.py:24
  113.0 6.3 %all-gather.5 = f32[32,2,128]{2,1,0:T(2,128)S(1)} all-gather(f32[8,2,128]{2,1,0:T(2,128)S(1)} %pad_maximum_fusion.30), channel_id=7, replica_groups=mesh['basin'=2,'row'=4,'col'=2,'sub'=2] {'col','sub'}, dimensions={0}, use_global_device_ids=true | all-gather | bytes 40960 | tf_op jit(solution)/shard_map/all_gather | solution.py:67
  121.3 3.8 %collective-permute-start.10 = (f32[1,32,2,128]{3,2,1,0:T(2,128)S(1)}, f32[1,32,2,128]{3,2,1,0:T(2,128)S(1)}, u32[]{:S(2)}, u32[]{:S(2)}) collective-permute-start(f32[1,32,2,128]{3,2,1,0:T(2,128)S(1)} %bitcast.569), channel_id=1, source_target_pairs={{0,4},{4,8},{8,12},{1,5},{5,9},{9,13},{2,6},{6,10},{10,14},{3,7},{... | collective-permute-start | bytes 98312 | tf_op jit(solution)/shard_map/ppermute | solution.py:24
  132.8 5.5 %all-gather.6 = f32[32,2,128]{2,1,0:T(2,128)S(1)} all-gather(f32[8,2,128]{2,1,0:T(2,128)S(1)} %pad_maximum_fusion.31), channel_id=8, replica_groups=mesh['basin'=2,'row'=4,'col'=2,'sub'=2] {'col','sub'}, dimensions={0}, use_global_device_ids=true | all-gather | bytes 40960 | tf_op jit(solution)/shard_map/all_gather | solution.py:67
  140.1 3.6 %collective-permute-start.12 = (f32[1,32,2,128]{3,2,1,0:T(2,128)S(1)}, f32[1,32,2,128]{3,2,1,0:T(2,128)S(1)}, u32[]{:S(2)}, u32[]{:S(2)}) collective-permute-start(f32[1,32,2,128]{3,2,1,0:T(2,128)S(1)} %bitcast.584), channel_id=1, source_target_pairs={{0,4},{4,8},{8,12},{1,5},{5,9},{9,13},{2,6},{6,10},{10,14},{3,7},{... | collective-permute-start | bytes 98312 | tf_op jit(solution)/shard_map/ppermute | solution.py:24
  160.1 34.1 %all-gather.16.cloned.1.call-done = f32[16,5,128,128]{3,2,1,0:T(8,128)} async-done(((f32[4,5,128,128]{3,2,1,0:T(8,128)}), f32[16,5,128,128]{3,2,1,0:T(8,128)}) %all-gather.16.cloned.1.call-update) | async-done | bytes 5242896 | tf_op jit(solution)/shard_map/all_gather | solution.py:122
  194.2 4.8 %gather_fusion.31 = f32[8,5,128,128]{3,2,1,0:T(8,128)} fusion(f32[16,5,128,128]{3,2,1,0:T(8,128)} %all-gather.16.cloned.1.call-done, s32[1024]{0:T(1024)S(1)} %pad_clamp_fusion.4), kind=kCustom, calls=%fused_computation.31 | custom fusion | bytes 5242912 | tf_op jit(solution)/shard_map/gather | solution.py:125
  204.2 5.3 %all-gather.8 = f32[32,2,128]{2,1,0:T(2,128)S(1)} all-gather(f32[8,2,128]{2,1,0:T(2,128)S(1)} %pad_maximum_fusion.32), channel_id=10, replica_groups=mesh['basin'=2,'row'=4,'col'=2,'sub'=2] {'col','sub'}, dimensions={0}, use_global_device_ids=true | all-gather | bytes 40960 | tf_op jit(solution)/shard_map/all_gather | solution.py:67
  220.8 3.5 %select_select_fusion.6 = (f32[8,128,128]{2,1,0:T(8,128)S(1)}, f32[8,128,128]{2,1,0:T(8,128)}, f32[8,128,128]{2,1,0:T(8,128)S(1)}, f32[8,128,128]{2,1,0:T(8,128)}) fusion(f32[8,5,128,128]{3,2,1,0:T(8,128)S(1)} %select_select_fusion, f32[8,128,1]{2,1,0:T(8,128)} %copy.392, f32[8,128,127]{2,1,0:T(8,128)} %slice.381, pred[8]{0:T(512)(128)(4,1)S(1)} %gather_fusion.1, ...), kind=kLoop, calls=%fused_computation.128 | loop fusion | flops 5373952 | bytes 6817800 | tf_op jit(solution)/shard_map/jit(_where)/select_n | solution.py:162
  225.5 5.8 %all-gather.9 = f32[32,2,128]{2,1,0:T(2,128)S(1)} all-gather(f32[8,2,128]{2,1,0:T(2,128)S(1)} %pad_maximum_fusion.33), channel_id=11, replica_groups=mesh['basin'=2,'row'=4,'col'=2,'sub'=2] {'col','sub'}, dimensions={0}, use_global_device_ids=true | all-gather | bytes 40960 | tf_op jit(solution)/shard_map/all_gather | solution.py:67
  233.4 3.1 collective-permute-start.16
  245.0 6.6 %all-gather.10 = f32[32,2,128]{2,1,0:T(2,128)S(1)} all-gather(f32[8,2,128]{2,1,0:T(2,128)S(1)} %pad_maximum_fusion.34), channel_id=12, replica_groups=mesh['basin'=2,'row'=4,'col'=2,'sub'=2] {'col','sub'}, dimensions={0}, use_global_device_ids=true | all-gather | bytes 40960 | tf_op jit(solution)/shard_map/all_gather | solution.py:67
  253.5 3.4 %collective-permute-start.18 = (f32[1,32,2,128]{3,2,1,0:T(2,128)S(1)}, f32[1,32,2,128]{3,2,1,0:T(2,128)S(1)}, u32[]{:S(2)}, u32[]{:S(2)}) collective-permute-start(f32[1,32,2,128]{3,2,1,0:T(2,128)S(1)} %bitcast.578), channel_id=1, source_target_pairs={{0,4},{4,8},{8,12},{1,5},{5,9},{9,13},{2,6},{6,10},{10,14},{3,7},{... | collective-permute-start | bytes 98312 | tf_op jit(solution)/shard_map/ppermute | solution.py:24
  263.1 3.4 %select_select_fusion.4 = (f32[8,128,128]{2,1,0:T(8,128)S(1)}, f32[8,128,128]{2,1,0:T(8,128)S(1)}) fusion(f32[8,128,128]{2,1,0:T(8,128)} %copy-done.1, f32[8,128,128]{2,1,0:T(8,128)} %get-tuple-element.8, f32[8,128,128]{2,1,0:T(8,128)} %get-tuple-element.14, f32[8,128,1]{2,1,0:T(8,128)} %copy.399, f32[8,128,127]{2,1,0:T(8,128)} %slice.393, ...), kind=kLoop, calls=%fused_computation.126 | loop fusion | flops 4718592 | bytes 5244936 | tf_op jit(solution)/shard_map/jit(_where)/select_n | solution.py:162
  267.7 5.8 %all-gather.11 = f32[32,2,128]{2,1,0:T(2,128)S(1)} all-gather(f32[8,2,128]{2,1,0:T(2,128)S(1)} %pad_maximum_fusion.35), channel_id=13, replica_groups=mesh['basin'=2,'row'=4,'col'=2,'sub'=2] {'col','sub'}, dimensions={0}, use_global_device_ids=true | all-gather | bytes 40960 | tf_op jit(solution)/shard_map/all_gather | solution.py:67
  275.4 3.6 %collective-permute-start.20 = (f32[1,32,2,128]{3,2,1,0:T(2,128)S(1)}, f32[1,32,2,128]{3,2,1,0:T(2,128)S(1)}, u32[]{:S(2)}, u32[]{:S(2)}) collective-permute-start(f32[1,32,2,128]{3,2,1,0:T(2,128)S(1)} %bitcast.587), channel_id=1, source_target_pairs={{0,4},{4,8},{8,12},{1,5},{5,9},{9,13},{2,6},{6,10},{10,14},{3,7},{... | collective-permute-start | bytes 98312 | tf_op jit(solution)/shard_map/ppermute | solution.py:24
  287.1 6.3 %all-gather.12 = f32[32,2,128]{2,1,0:T(2,128)S(1)} all-gather(f32[8,2,128]{2,1,0:T(2,128)S(1)} %pad_maximum_fusion.36), channel_id=14, replica_groups=mesh['basin'=2,'row'=4,'col'=2,'sub'=2] {'col','sub'}, dimensions={0}, use_global_device_ids=true | all-gather | bytes 40960 | tf_op jit(solution)/shard_map/all_gather | solution.py:67
  295.4 3.6 %collective-permute-start.22 = (f32[1,32,2,128]{3,2,1,0:T(2,128)S(1)}, f32[1,32,2,128]{3,2,1,0:T(2,128)S(1)}, u32[]{:S(2)}, u32[]{:S(2)}) collective-permute-start(f32[1,32,2,128]{3,2,1,0:T(2,128)S(1)} %bitcast.581), channel_id=1, source_target_pairs={{0,4},{4,8},{8,12},{1,5},{5,9},{9,13},{2,6},{6,10},{10,14},{3,7},{... | collective-permute-start | bytes 98312 | tf_op jit(solution)/shard_map/ppermute | solution.py:24
  305.2 3.3 select_select_fusion.2
  309.7 5.5 %all-gather.13 = f32[32,2,128]{2,1,0:T(2,128)S(1)} all-gather(f32[8,2,128]{2,1,0:T(2,128)S(1)} %pad_maximum_fusion.37), channel_id=15, replica_groups=mesh['basin'=2,'row'=4,'col'=2,'sub'=2] {'col','sub'}, dimensions={0}, use_global_device_ids=true | all-gather | bytes 40960 | tf_op jit(solution)/shard_map/all_gather | solution.py:67
  317.1 3.6 %collective-permute-start.24 = (f32[1,32,2,128]{3,2,1,0:T(2,128)S(1)}, f32[1,32,2,128]{3,2,1,0:T(2,128)S(1)}, u32[]{:S(2)}, u32[]{:S(2)}) collective-permute-start(f32[1,32,2,128]{3,2,1,0:T(2,128)S(1)} %bitcast.590), channel_id=1, source_target_pairs={{0,4},{4,8},{8,12},{1,5},{5,9},{9,13},{2,6},{6,10},{10,14},{3,7},{... | collective-permute-start | bytes 98312 | tf_op jit(solution)/shard_map/ppermute | solution.py:24
  (304 shorter events, 143.8 us)
Async XLA Ops:
  7.2 187.1 %all-gather.16.cloned.1.call-start = ((), (), s32[]{:S(2)}) async-start(), calls=%async_computation | async-start | bytes 6553600 | tf_op jit(solution)/shard_map/all_gather | solution.py:122
  14.9 38.2 %collective-permute-start.1 = (f32[1,32,2,128]{3,2,1,0:T(2,128)S(1)}, f32[1,32,2,128]{3,2,1,0:T(2,128)S(1)}, u32[]{:S(2)}, u32[]{:S(2)}) collective-permute-start(f32[1,32,2,128]{3,2,1,0:T(2,128)S(1)} %bitcast.553), channel_id=1, source_target_pairs={{4,0},{8,4},{12,8},{5,1},{9,5},{13,9},{6,2},{10,6},{14,10},{7,3},{... | collective-permute-start | bytes 98312 | tf_op jit(solution)/shard_map/ppermute | solution.py:25
  16.8 36.3 %collective-permute-start = (f32[1,32,2,128]{3,2,1,0:T(2,128)S(1)}, f32[1,32,2,128]{3,2,1,0:T(2,128)S(1)}, u32[]{:S(2)}, u32[]{:S(2)}) collective-permute-start(f32[1,32,2,128]{3,2,1,0:T(2,128)S(1)} %bitcast.554), channel_id=1, source_target_pairs={{0,4},{4,8},{8,12},{1,5},{5,9},{9,13},{2,6},{6,10},{10,14},{3,7},{... | collective-permute-start | bytes 98312 | tf_op jit(solution)/shard_map/ppermute | solution.py:24
  27.9 25.8 %collective-permute-start.3 = (f32[1,32,2,128]{3,2,1,0:T(2,128)S(1)}, f32[1,32,2,128]{3,2,1,0:T(2,128)S(1)}, u32[]{:S(2)}, u32[]{:S(2)}) collective-permute-start(f32[1,32,2,128]{3,2,1,0:T(2,128)S(1)} %bitcast.556), channel_id=1, source_target_pairs={{4,0},{8,4},{12,8},{5,1},{9,5},{13,9},{6,2},{10,6},{14,10},{7,3},{... | collective-permute-start | bytes 98312 | tf_op jit(solution)/shard_map/ppermute | solution.py:25
  29.9 23.9 %collective-permute-start.2 = (f32[1,32,2,128]{3,2,1,0:T(2,128)S(1)}, f32[1,32,2,128]{3,2,1,0:T(2,128)S(1)}, u32[]{:S(2)}, u32[]{:S(2)}) collective-permute-start(f32[1,32,2,128]{3,2,1,0:T(2,128)S(1)} %bitcast.557), channel_id=1, source_target_pairs={{0,4},{4,8},{8,12},{1,5},{5,9},{9,13},{2,6},{6,10},{10,14},{3,7},{... | collective-permute-start | bytes 98312 | tf_op jit(solution)/shard_map/ppermute | solution.py:24
  41.5 8.5 %copy-start = (f32[8,128,128]{2,1,0:T(8,128)S(1)}, f32[8,128,128]{2,1,0:T(8,128)}, u32[]{:S(2)}) copy-start(f32[8,128,128]{2,1,0:T(8,128)} %param.11) | copy-start | bytes 1572868
  61.2 15.2 %copy-start.9 = (f32[8,128,128]{2,1,0:T(8,128)S(1)}, f32[8,128,128]{2,1,0:T(8,128)}, u32[]{:S(2)}) copy-start(f32[8,128,128]{2,1,0:T(8,128)} %param.8) | copy-start | bytes 1572868
  67.4 5.4 %collective-permute-start.5 = (f32[1,32,2,128]{3,2,1,0:T(2,128)S(1)}, f32[1,32,2,128]{3,2,1,0:T(2,128)S(1)}, u32[]{:S(2)}, u32[]{:S(2)}) collective-permute-start(f32[1,32,2,128]{3,2,1,0:T(2,128)S(1)} %bitcast.559), channel_id=1, source_target_pairs={{4,0},{8,4},{12,8},{5,1},{9,5},{13,9},{6,2},{10,6},{14,10},{7,3},{... | collective-permute-start | bytes 98312 | tf_op jit(solution)/shard_map/ppermute | solution.py:25
  69.3 4.7 %collective-permute-start.4 = (f32[1,32,2,128]{3,2,1,0:T(2,128)S(1)}, f32[1,32,2,128]{3,2,1,0:T(2,128)S(1)}, u32[]{:S(2)}, u32[]{:S(2)}) collective-permute-start(f32[1,32,2,128]{3,2,1,0:T(2,128)S(1)} %bitcast.560), channel_id=1, source_target_pairs={{0,4},{4,8},{8,12},{1,5},{5,9},{9,13},{2,6},{6,10},{10,14},{3,7},{... | collective-permute-start | bytes 98312 | tf_op jit(solution)/shard_map/ppermute | solution.py:24
  77.8 16.5 %copy-start.12 = (f32[8,128,128]{2,1,0:T(8,128)}, f32[8,128,128]{2,1,0:T(8,128)S(1)}, u32[]{:S(2)}) copy-start(f32[8,128,128]{2,1,0:T(8,128)S(1)} %get-tuple-element.22) | copy-start | bytes 1572868
  84.3 7.6 %collective-permute-start.7 = (f32[1,32,2,128]{3,2,1,0:T(2,128)S(1)}, f32[1,32,2,128]{3,2,1,0:T(2,128)S(1)}, u32[]{:S(2)}, u32[]{:S(2)}) collective-permute-start(f32[1,32,2,128]{3,2,1,0:T(2,128)S(1)} %bitcast.565), channel_id=1, source_target_pairs={{4,0},{8,4},{12,8},{5,1},{9,5},{13,9},{6,2},{10,6},{14,10},{7,3},{... | collective-permute-start | bytes 98312 | tf_op jit(solution)/shard_map/ppermute | solution.py:25
  86.3 5.7 %collective-permute-start.6 = (f32[1,32,2,128]{3,2,1,0:T(2,128)S(1)}, f32[1,32,2,128]{3,2,1,0:T(2,128)S(1)}, u32[]{:S(2)}, u32[]{:S(2)}) collective-permute-start(f32[1,32,2,128]{3,2,1,0:T(2,128)S(1)} %bitcast.566), channel_id=1, source_target_pairs={{0,4},{4,8},{8,12},{1,5},{5,9},{9,13},{2,6},{6,10},{10,14},{3,7},{... | collective-permute-start | bytes 98312 | tf_op jit(solution)/shard_map/ppermute | solution.py:24
  103.2 5.7 %collective-permute-start.9 = (f32[1,32,2,128]{3,2,1,0:T(2,128)S(1)}, f32[1,32,2,128]{3,2,1,0:T(2,128)S(1)}, u32[]{:S(2)}, u32[]{:S(2)}) collective-permute-start(f32[1,32,2,128]{3,2,1,0:T(2,128)S(1)} %bitcast.571), channel_id=1, source_target_pairs={{4,0},{8,4},{12,8},{5,1},{9,5},{13,9},{6,2},{10,6},{14,10},{7,3},{... | collective-permute-start | bytes 98312 | tf_op jit(solution)/shard_map/ppermute | solution.py:25
  105.1 4.7 %collective-permute-start.8 = (f32[1,32,2,128]{3,2,1,0:T(2,128)S(1)}, f32[1,32,2,128]{3,2,1,0:T(2,128)S(1)}, u32[]{:S(2)}, u32[]{:S(2)}) collective-permute-start(f32[1,32,2,128]{3,2,1,0:T(2,128)S(1)} %bitcast.572), channel_id=1, source_target_pairs={{0,4},{4,8},{8,12},{1,5},{5,9},{9,13},{2,6},{6,10},{10,14},{3,7},{... | collective-permute-start | bytes 98312 | tf_op jit(solution)/shard_map/ppermute | solution.py:24
  112.8 16.4 %copy-start.10 = (f32[8,128,128]{2,1,0:T(8,128)}, f32[8,128,128]{2,1,0:T(8,128)S(1)}, u32[]{:S(2)}) copy-start(f32[8,128,128]{2,1,0:T(8,128)S(1)} %get-tuple-element.20) | copy-start | bytes 1572868
  119.4 7.6 %collective-permute-start.11 = (f32[1,32,2,128]{3,2,1,0:T(2,128)S(1)}, f32[1,32,2,128]{3,2,1,0:T(2,128)S(1)}, u32[]{:S(2)}, u32[]{:S(2)}) collective-permute-start(f32[1,32,2,128]{3,2,1,0:T(2,128)S(1)} %bitcast.568), channel_id=1, source_target_pairs={{4,0},{8,4},{12,8},{5,1},{9,5},{13,9},{6,2},{10,6},{14,10},{7,3},{... | collective-permute-start | bytes 98312 | tf_op jit(solution)/shard_map/ppermute | solution.py:25
  121.3 5.7 %collective-permute-start.10 = (f32[1,32,2,128]{3,2,1,0:T(2,128)S(1)}, f32[1,32,2,128]{3,2,1,0:T(2,128)S(1)}, u32[]{:S(2)}, u32[]{:S(2)}) collective-permute-start(f32[1,32,2,128]{3,2,1,0:T(2,128)S(1)} %bitcast.569), channel_id=1, source_target_pairs={{0,4},{4,8},{8,12},{1,5},{5,9},{9,13},{2,6},{6,10},{10,14},{3,7},{... | collective-permute-start | bytes 98312 | tf_op jit(solution)/shard_map/ppermute | solution.py:24
  138.2 5.6 %collective-permute-start.13 = (f32[1,32,2,128]{3,2,1,0:T(2,128)S(1)}, f32[1,32,2,128]{3,2,1,0:T(2,128)S(1)}, u32[]{:S(2)}, u32[]{:S(2)}) collective-permute-start(f32[1,32,2,128]{3,2,1,0:T(2,128)S(1)} %bitcast.583), channel_id=1, source_target_pairs={{4,0},{8,4},{12,8},{5,1},{9,5},{13,9},{6,2},{10,6},{14,10},{7,3},{... | collective-permute-start | bytes 98312 | tf_op jit(solution)/shard_map/ppermute | solution.py:25
  140.1 4.7 %collective-permute-start.12 = (f32[1,32,2,128]{3,2,1,0:T(2,128)S(1)}, f32[1,32,2,128]{3,2,1,0:T(2,128)S(1)}, u32[]{:S(2)}, u32[]{:S(2)}) collective-permute-start(f32[1,32,2,128]{3,2,1,0:T(2,128)S(1)} %bitcast.584), channel_id=1, source_target_pairs={{0,4},{4,8},{8,12},{1,5},{5,9},{9,13},{2,6},{6,10},{10,14},{3,7},{... | collective-permute-start | bytes 98312 | tf_op jit(solution)/shard_map/ppermute | solution.py:24
  209.5 9.0 %collective-permute-start.15 = (f32[1,32,2,128]{3,2,1,0:T(2,128)S(1)}, f32[1,32,2,128]{3,2,1,0:T(2,128)S(1)}, u32[]{:S(2)}, u32[]{:S(2)}) collective-permute-start(f32[1,32,2,128]{3,2,1,0:T(2,128)S(1)} %bitcast.562), channel_id=1, source_target_pairs={{4,0},{8,4},{12,8},{5,1},{9,5},{13,9},{6,2},{10,6},{14,10},{7,3},{... | collective-permute-start | bytes 98312 | tf_op jit(solution)/shard_map/ppermute | solution.py:25
  211.7 6.9 %collective-permute-start.14 = (f32[1,32,2,128]{3,2,1,0:T(2,128)S(1)}, f32[1,32,2,128]{3,2,1,0:T(2,128)S(1)}, u32[]{:S(2)}, u32[]{:S(2)}) collective-permute-start(f32[1,32,2,128]{3,2,1,0:T(2,128)S(1)} %bitcast.563), channel_id=1, source_target_pairs={{0,4},{4,8},{8,12},{1,5},{5,9},{9,13},{2,6},{6,10},{10,14},{3,7},{... | collective-permute-start | bytes 98312 | tf_op jit(solution)/shard_map/ppermute | solution.py:24
  224.3 18.6 %copy-start.1 = (f32[8,128,128]{2,1,0:T(8,128)}, f32[8,128,128]{2,1,0:T(8,128)S(1)}, u32[]{:S(2)}) copy-start(f32[8,128,128]{2,1,0:T(8,128)S(1)} %get-tuple-element.13) | copy-start | bytes 1572868
  231.3 5.3 %collective-permute-start.17 = (f32[1,32,2,128]{3,2,1,0:T(2,128)S(1)}, f32[1,32,2,128]{3,2,1,0:T(2,128)S(1)}, u32[]{:S(2)}, u32[]{:S(2)}) collective-permute-start(f32[1,32,2,128]{3,2,1,0:T(2,128)S(1)} %bitcast.574), channel_id=1, source_target_pairs={{4,0},{8,4},{12,8},{5,1},{9,5},{13,9},{6,2},{10,6},{14,10},{7,3},{... | collective-permute-start | bytes 98312 | tf_op jit(solution)/shard_map/ppermute | solution.py:25
  233.4 4.7 %collective-permute-start.16 = (f32[1,32,2,128]{3,2,1,0:T(2,128)S(1)}, f32[1,32,2,128]{3,2,1,0:T(2,128)S(1)}, u32[]{:S(2)}, u32[]{:S(2)}) collective-permute-start(f32[1,32,2,128]{3,2,1,0:T(2,128)S(1)} %bitcast.575), channel_id=1, source_target_pairs={{0,4},{4,8},{8,12},{1,5},{5,9},{9,13},{2,6},{6,10},{10,14},{3,7},{... | collective-permute-start | bytes 98312 | tf_op jit(solution)/shard_map/ppermute | solution.py:24
  251.6 9.2 %collective-permute-start.19 = (f32[1,32,2,128]{3,2,1,0:T(2,128)S(1)}, f32[1,32,2,128]{3,2,1,0:T(2,128)S(1)}, u32[]{:S(2)}, u32[]{:S(2)}) collective-permute-start(f32[1,32,2,128]{3,2,1,0:T(2,128)S(1)} %bitcast.577), channel_id=1, source_target_pairs={{4,0},{8,4},{12,8},{5,1},{9,5},{13,9},{6,2},{10,6},{14,10},{7,3},{... | collective-permute-start | bytes 98312 | tf_op jit(solution)/shard_map/ppermute | solution.py:25
  253.5 7.3 %collective-permute-start.18 = (f32[1,32,2,128]{3,2,1,0:T(2,128)S(1)}, f32[1,32,2,128]{3,2,1,0:T(2,128)S(1)}, u32[]{:S(2)}, u32[]{:S(2)}) collective-permute-start(f32[1,32,2,128]{3,2,1,0:T(2,128)S(1)} %bitcast.578), channel_id=1, source_target_pairs={{0,4},{4,8},{8,12},{1,5},{5,9},{9,13},{2,6},{6,10},{10,14},{3,7},{... | collective-permute-start | bytes 98312 | tf_op jit(solution)/shard_map/ppermute | solution.py:24
  273.5 5.5 %collective-permute-start.21 = (f32[1,32,2,128]{3,2,1,0:T(2,128)S(1)}, f32[1,32,2,128]{3,2,1,0:T(2,128)S(1)}, u32[]{:S(2)}, u32[]{:S(2)}) collective-permute-start(f32[1,32,2,128]{3,2,1,0:T(2,128)S(1)} %bitcast.586), channel_id=1, source_target_pairs={{4,0},{8,4},{12,8},{5,1},{9,5},{13,9},{6,2},{10,6},{14,10},{7,3},{... | collective-permute-start | bytes 98312 | tf_op jit(solution)/shard_map/ppermute | solution.py:25
  275.4 4.7 %collective-permute-start.20 = (f32[1,32,2,128]{3,2,1,0:T(2,128)S(1)}, f32[1,32,2,128]{3,2,1,0:T(2,128)S(1)}, u32[]{:S(2)}, u32[]{:S(2)}) collective-permute-start(f32[1,32,2,128]{3,2,1,0:T(2,128)S(1)} %bitcast.587), channel_id=1, source_target_pairs={{0,4},{4,8},{8,12},{1,5},{5,9},{9,13},{2,6},{6,10},{10,14},{3,7},{... | collective-permute-start | bytes 98312 | tf_op jit(solution)/shard_map/ppermute | solution.py:24
  293.5 9.5 %collective-permute-start.23 = (f32[1,32,2,128]{3,2,1,0:T(2,128)S(1)}, f32[1,32,2,128]{3,2,1,0:T(2,128)S(1)}, u32[]{:S(2)}, u32[]{:S(2)}) collective-permute-start(f32[1,32,2,128]{3,2,1,0:T(2,128)S(1)} %bitcast.580), channel_id=1, source_target_pairs={{4,0},{8,4},{12,8},{5,1},{9,5},{13,9},{6,2},{10,6},{14,10},{7,3},{... | collective-permute-start | bytes 98312 | tf_op jit(solution)/shard_map/ppermute | solution.py:25
  295.4 7.6 %collective-permute-start.22 = (f32[1,32,2,128]{3,2,1,0:T(2,128)S(1)}, f32[1,32,2,128]{3,2,1,0:T(2,128)S(1)}, u32[]{:S(2)}, u32[]{:S(2)}) collective-permute-start(f32[1,32,2,128]{3,2,1,0:T(2,128)S(1)} %bitcast.581), channel_id=1, source_target_pairs={{0,4},{4,8},{8,12},{1,5},{5,9},{9,13},{2,6},{6,10},{10,14},{3,7},{... | collective-permute-start | bytes 98312 | tf_op jit(solution)/shard_map/ppermute | solution.py:24
  315.2 5.6 %collective-permute-start.25 = (f32[1,32,2,128]{3,2,1,0:T(2,128)S(1)}, f32[1,32,2,128]{3,2,1,0:T(2,128)S(1)}, u32[]{:S(2)}, u32[]{:S(2)}) collective-permute-start(f32[1,32,2,128]{3,2,1,0:T(2,128)S(1)} %bitcast.589), channel_id=1, source_target_pairs={{4,0},{8,4},{12,8},{5,1},{9,5},{13,9},{6,2},{10,6},{14,10},{7,3},{... | collective-permute-start | bytes 98312 | tf_op jit(solution)/shard_map/ppermute | solution.py:25
  317.1 4.7 %collective-permute-start.24 = (f32[1,32,2,128]{3,2,1,0:T(2,128)S(1)}, f32[1,32,2,128]{3,2,1,0:T(2,128)S(1)}, u32[]{:S(2)}, u32[]{:S(2)}) collective-permute-start(f32[1,32,2,128]{3,2,1,0:T(2,128)S(1)} %bitcast.590), channel_id=1, source_target_pairs={{0,4},{4,8},{8,12},{1,5},{5,9},{9,13},{2,6},{6,10},{10,14},{3,7},{... | collective-permute-start | bytes 98312 | tf_op jit(solution)/shard_map/ppermute | solution.py:24
  (10 other events, 23.3 us)
Sparse Core Ops, SparseCore 0:
  150.2 43.9 all-gather.15
where the time goes:
time: 336 us; the launch traced here: 333 us
  local copies, waits for them, and re-layouts  91.3 us (27%)
  blocking collectives  76 us (23%)
  starting transfers between devices  70.6 us (21%)
  waiting for transfers between devices  40.8 us (12%)
  other arithmetic  39.1 us (12%)
  between operations  15.1 us (4%)
    all_gather x13, blocking collectives, share_edges(): lax.all_gather(edge_rows[None], ('col', 'sub'), axis=1, tiled=True)  76 us
    ppermute x13, starting transfers between devices, padded(): before = lax.ppermute(last, axis, up)  45.3 us
    all_gather x1, waiting for transfers between devices, shards(): lax.all_gather(stacked[chosen_slots], ('col', 'sub'), axis=0, tiled=True)  34.1 us
    ppermute x13, starting transfers between devices, padded(): after = lax.ppermute(first, axis, down)  25.3 us
    select_n x6, other arithmetic, shards(): flow_x = jnp.where(wet_cells, jnp.where(open_x, updated_x, 0.0), flow_x)  20.1 us
    unnamed x41, local copies, waits for them, and re-layouts  11.5 us
    slice x6, local copies, waits for them, and re-layouts, shards(): surface[:, :, 1:]  8.08 us
    add x6, other arithmetic, shards(): surface = depth_now + ground  8 us
  transfers between devices with their start and end apart: 27, of which 7 were waited for; matrix products, arithmetic and copies ran while one was open for 14% of the time, Pallas kernels for 0%

commit v1 on v0

v1 whole, which is shorter than its diff:
```python
import functools
import jax
import jax.numpy as jnp
from jax import lax
from jax.experimental import pallas as pl
from jax.experimental.pallas import tpu as pltpu
from jax.sharding import PartitionSpec as P

STEPS = 6
HALO = 6
MOVE = 4
PER_PEER = 2
GRAV = 9.81
STEP_TIME = 0.5
SPACING = 5.0
RATE = 0.1
DEPTH_FLOOR = 0.3
CLOSED = 1e30
SUBL = 8
LANE = 128
SEG = 12
HALF = 64
REC = 32
MESH_ID = pl.DeviceIdType.MESH
VMEM_LIMIT = 40 * 1024 * 1024

DIRS = ((0, -1), (0, 1), (-1, 0), (-1, -1), (-1, 1), (1, 0), (1, -1), (1, 1))


def table_kernel(tiles, lanes, rows, me_ref, pb_ref, pa_ref, wet_ref, tbl_ref, invb, inva, cnt):
    total = lanes * rows * tiles
    row_tiles = lanes * tiles
    my_row = me_ref[0]
    my_lane = me_ref[1]
    my_dev = my_row * lanes + my_lane

    def fill(s, _):
        invb[pb_ref[s]] = s
        inva[pa_ref[s]] = s
        return 0

    lax.fori_loop(0, total, fill, 0)
    for o in range(lanes):
        cnt[o] = 0

    def place(t, ranks):
        leave_rank, stay_rank = ranks
        tile = pb_ref[my_dev * tiles + t]
        dest = inva[tile] // tiles
        leaving = dest != my_dev
        pos = jnp.where(leaving, leave_rank, stay_rank)
        base = pos * REC
        tbl_ref[base] = t
        tbl_ref[base + 1] = wet_ref[tile]
        trow = tile // row_tiles
        tcol = tile % row_tiles
        for d, (dr, dc) in enumerate(DIRS):
            r, c = trow + dr, tcol + dc
            exists = (r >= 0) & (r < rows) & (c >= 0) & (c < row_tiles)
            other = jnp.where(exists, r * row_tiles + c, 0)
            where = invb[other] % row_tiles
            tbl_ref[base + 2 + d] = jnp.where(exists, wet_ref[other], 0)
            tbl_ref[base + 10 + 2 * d] = where // tiles
            tbl_ref[base + 11 + 2 * d] = where % tiles
        off = lax.rem(dest % lanes - my_lane + lanes, lanes)
        k = cnt[off]
        cnt[off] = k + 1
        tbl_ref[base + 26] = off
        tbl_ref[base + 27] = k
        lv = leaving.astype(jnp.int32)
        return leave_rank + lv, stay_rank + 1 - lv

    lax.fori_loop(0, tiles, place, (jnp.int32(0), jnp.int32(MOVE)))

    def final(s, _):
        src = invb[pa_ref[my_dev * tiles + s]]
        src_dev = src // tiles
        off = lax.rem(my_lane - src_dev % lanes + lanes, lanes)

        def rank(j, n):
            same = (inva[pb_ref[src_dev * tiles + j]] // tiles == my_dev) & (j < src % tiles)
            return n + same.astype(jnp.int32)

        n = lax.fori_loop(0, tiles, rank, jnp.int32(0))
        tbl_ref[tiles * REC + 2 * s] = off
        tbl_ref[tiles * REC + 2 * s + 1] = n
        return 0

    lax.fori_loop(0, tiles, final, 0)


def halo_kernel(tiles, h, x, y, z, m, gc, gu, gd, top, bot, ssem, rsem, vs, vr):
    cols = lax.axis_size("col")
    rows = lax.axis_size("row")
    b = lax.axis_index("basin")
    r = lax.axis_index("row")
    c = lax.axis_index("col")
    s = lax.axis_index("sub")
    other = 1 - s
    me = c * 2 + s
    sib = c * 2 + other
    fields = (h, x, y, z, m)

    barrier = pltpu.get_barrier_semaphore()
    pl.semaphore_signal(barrier, inc=1, device_id=(b, r, c, other), device_id_type=MESH_ID)
    for d in range(1, cols):
        pl.semaphore_signal(
            barrier, inc=1, device_id=(b, r, lax.rem(c + d, cols), s), device_id_type=MESH_ID
        )

    @pl.when(r > 0)
    def _():
        pl.semaphore_signal(barrier, inc=1, device_id=(b, r - 1, c, s), device_id_type=MESH_ID)

    @pl.when(r < rows - 1)
    def _():
        pl.semaphore_signal(barrier, inc=1, device_id=(b, r + 1, c, s), device_id_type=MESH_ID)

    for f in range(5):
        top[:, f] = fields[f][:, 0:SUBL, :]
        bot[:, f] = fields[f][:, LANE - SUBL : LANE, :]

    beside = jnp.where(r > 0, 1, 0) + jnp.where(r < rows - 1, 1, 0)
    pl.semaphore_wait(barrier, cols + beside)

    def up_copy():
        return pltpu.make_async_remote_copy(
            top, gd.at[me], vs.at[0], vr.at[0], device_id=(b, r - 1, c, s), device_id_type=MESH_ID
        )

    def down_copy():
        return pltpu.make_async_remote_copy(
            bot, gu.at[me], vs.at[1], vr.at[1], device_id=(b, r + 1, c, s), device_id_type=MESH_ID
        )

    @pl.when(r > 0)
    def _():
        up_copy().start()

    @pl.when(r < rows - 1)
    def _():
        down_copy().start()

    lane = lax.broadcasted_iota(jnp.int32, (SUBL, LANE), 1)

    def pack(i, _):
        blk = i // (LANE // SUBL)
        row = pl.multiple_of((i % (LANE // SUBL)) * SUBL, SUBL)
        acc = jnp.zeros((SUBL, LANE), jnp.float32)
        for u in range(2):
            for f in range(5):
                base = u * HALF + f * SEG
                v = fields[f][2 * blk + u, pl.ds(row, SUBL), :]
                v = pltpu.roll(v, (base - (LANE - HALO)) % LANE, 1)
                acc = jnp.where((lane >= base) & (lane < base + SEG), v, acc)
        gc[me, blk, pl.ds(row, SUBL), :] = acc
        return 0

    lax.fori_loop(0, (tiles // 2) * (LANE // SUBL), pack, 0)

    bufs = (gc, gu, gd)

    def across(kind, d):
        return pltpu.make_async_remote_copy(
            bufs[kind].at[me],
            bufs[kind].at[me],
            ssem.at[kind, d],
            rsem.at[kind, me],
            device_id=(b, r, lax.rem(c + d, cols), s),
            device_id_type=MESH_ID,
        )

    def sideways(kind, src_col, d):
        slot = src_col * 2 + s
        return pltpu.make_async_remote_copy(
            bufs[kind].at[slot],
            bufs[kind].at[slot],
            ssem.at[kind, cols + d],
            rsem.at[kind, slot],
            device_id=(b, r, c, other),
            device_id_type=MESH_ID,
        )

    def arrived(kind, slot):
        pltpu.make_async_remote_copy(
            bufs[kind].at[slot],
            bufs[kind].at[slot],
            ssem.at[kind, 0],
            rsem.at[kind, slot],
            device_id=(b, r, c, other),
            device_id_type=MESH_ID,
        ).wait_recv()

    def spread(kind):
        for d in range(1, cols):
            across(kind, d).start()
        sideways(kind, c, 0).start()

    def relay(kind):
        for d in range(1, cols):
            src = lax.rem(c + d, cols)
            arrived(kind, src * 2 + s)
            sideways(kind, src, d).start()

    def close(kind):
        for d in range(cols):
            src = lax.rem(c + d, cols)
            arrived(kind, src * 2 + other)
        for d in range(1, cols):
            across(kind, d).wait_send()
        for d in range(cols):
            sideways(kind, lax.rem(c + d, cols), d).wait_send()

    spread(0)

    @pl.when(r < rows - 1)
    def _():
        up_copy().wait_recv()
        spread(2)

    @pl.when(r > 0)
    def _():
        down_copy().wait_recv()
        spread(1)

    relay(0)

    @pl.when(r < rows - 1)
    def _():
        relay(2)

    @pl.when(r > 0)
    def _():
        relay(1)

    close(0)

    @pl.when(r < rows - 1)
    def _():
        close(2)
        down_copy().wait_send()

    @pl.when(r > 0)
    def _():
        close(1)
        up_copy().wait_send()


def steps_kernel(first, count, peers, tbl, h, x, y, z, m, gc, gu, gd, *rest):
    outs = rest[: max(peers, 1)]
    ph, px, py, pz, pm, mx, my, pw = rest[max(peers, 1) :]
    fields = (h, x, y, z, m)
    packs = (ph, px, py, pz, pm)
    width = ph.shape[1]
    nblk = width // LANE
    pitch = LANE + 2 * HALO
    nrow = LANE // SUBL
    chunks = nrow + 2
    lane = lax.broadcasted_iota(jnp.int32, (SUBL, LANE), 1)

    def put(acc, v, a, d, length):
        shift = (d - a) % LANE
        if shift:
            v = pltpu.roll(v, shift, 1)
        for k in range(d // LANE, (d + length - 1) // LANE + 1):
            lo = max(d - k * LANE, 0)
            hi = min(d + length - k * LANE, LANE)
            acc[k] = jnp.where((lane >= lo) & (lane < hi), v, acc[k])

    def rec(q, i):
        return tbl[(first + q) * REC + i]

    def fresh():
        return [jnp.zeros((SUBL, LANE), jnp.float32) for _ in range(nblk)]

    def save(ref, row, acc):
        ref[pl.ds(row, SUBL), :] = jnp.concatenate(acc, axis=1)

    def fill(i, _):
        row = pl.multiple_of(i * SUBL, SUBL)
        west, east = [], []
        for q in range(count):
            side = []
            for d in range(2):
                ln, sl = rec(q, 10 + 2 * d), rec(q, 11 + 2 * d)
                v = gc[ln, sl // 2, pl.ds(row, SUBL), :]
                v = jnp.where(sl % 2 == 1, pltpu.roll(v, HALF, 1), v)
                side.append(jnp.where(rec(q, 2 + d) == 1, v, 0.0))
            west.append(side[0])
            east.append(side[1])
        for f in range(5):
            acc = fresh()
            for q in range(count):
                at = q * pitch + HALO
                put(acc, fields[f][rec(q, 0), pl.ds(row, SUBL), :], 0, at, LANE)
                put(acc, west[q], f * SEG, at - HALO, HALO)
                put(acc, east[q], f * SEG + HALO, at + LANE, HALO)
            save(packs[f], row + SUBL, acc)
        return 0

    lax.fori_loop(0, nrow, fill, 0)
    for row, buf, d0 in ((0, gu, 2), (LANE + SUBL, gd, 5)):
        for f in range(5):
            acc = fresh()
            for q in range(count):
                at = q * pitch + HALO
                got = []
                for d in range(d0, d0 + 3):
                    v = buf[rec(q, 10 + 2 * d), rec(q, 11 + 2 * d), f]
                    got.append(jnp.where(rec(q, 2 + d) == 1, v, 0.0))
                put(acc, got[0], 0, at, LANE)
                put(acc, got[1], LANE - HALO, at - HALO, HALO)
                put(acc, got[2], 0, at + LANE, HALO)
            save(packs[f], row, acc)

    def wet_rows(cell, left, right):
        acc = fresh()
        for q in range(count):
            at = q * pitch + HALO
            for i, a, n in ((cell, at, LANE), (left, at - HALO, HALO), (right, at + LANE, HALO)):
                v = jnp.full((SUBL, LANE), (rec(q, i) == 1).astype(jnp.float32))
                put(acc, v, a, a, n)
        return jnp.concatenate(acc, axis=1)

    pw[0:SUBL, :] = wet_rows(4, 5, 6)
    pw[SUBL : 2 * SUBL, :] = wet_rows(1, 2, 3)
    pw[2 * SUBL : 3 * SUBL, :] = wet_rows(7, 8, 9)

    full = (SUBL, width)
    sub = lax.broadcasted_iota(jnp.int32, full, 0)
    last_row = sub == SUBL - 1
    first_row = sub == 0

    def ready(i, _):
        row = pl.multiple_of(i * SUBL, SUBL)
        nxt = pl.multiple_of(jnp.minimum(i + 1, chunks - 1) * SUBL, SUBL)
        kind = jnp.where(i == 0, 0, jnp.where(i == chunks - 1, 2, 1))
        kind2 = jnp.where(i + 1 >= chunks - 1, 2, 1)
        w = pw[pl.ds(pl.multiple_of(kind * SUBL, SUBL), SUBL), :]
        w2 = pw[pl.ds(pl.multiple_of(kind2 * SUBL, SUBL), SUBL), :]
        ww = pltpu.roll(w, width - 1, 1)
        ws = jnp.where(last_row, w2, w)
        zz = pz[pl.ds(row, SUBL), :]
        zn = pz[pl.ds(nxt, SUBL), :]
        ze = pltpu.roll(zz, width - 1, 1)
        zs = pltpu.roll(jnp.where(first_row, zn, zz), SUBL - 1, 0)
        ox = w * ww > 0.5
        oy = w * ws > 0.5
        mx[pl.ds(row, SUBL), :] = jnp.where(ox, jnp.maximum(zz, ze), CLOSED)
        my[pl.ds(row, SUBL), :] = jnp.where(oy, jnp.maximum(zz, zs), CLOSED)
        px[pl.ds(row, SUBL), :] = jnp.where(ox, px[pl.ds(row, SUBL), :], 0.0)
        py[pl.ds(row, SUBL), :] = jnp.where(oy, py[pl.ds(row, SUBL), :], 0.0)
        mm = pm[pl.ds(row, SUBL), :]
        pm[pl.ds(row, SUBL), :] = (GRAV * STEP_TIME) * mm * mm
        return 0

    lax.fori_loop(0, chunks, ready, 0)

    def face(q, e, e2, mz, mm):
        f = jnp.maximum(e, e2) - mz
        num = q - (GRAV * STEP_TIME / SPACING) * jnp.maximum(f, 0.0) * (e2 - e)
        g = jnp.exp((-7.0 / 3.0) * jnp.log(jnp.maximum(f, DEPTH_FLOOR)))
        return num / (1.0 + mm * jnp.abs(q) * g)

    def chunk(i, carry):
        e, qy_above = carry
        row = pl.multiple_of(i * SUBL, SUBL)
        nxt = pl.multiple_of(jnp.minimum(i + 1, chunks - 1) * SUBL, SUBL)
        en = ph[pl.ds(nxt, SUBL), :] + pz[pl.ds(nxt, SUBL), :]
        mm = pm[pl.ds(row, SUBL), :]
        ee = pltpu.roll(e, width - 1, 1)
        es = pltpu.roll(jnp.where(first_row, en, e), SUBL - 1, 0)
        qx = face(px[pl.ds(row, SUBL), :], e, ee, mx[pl.ds(row, SUBL), :], mm)
        px[pl.ds(row, SUBL), :] = qx
        qy = face(py[pl.ds(row, SUBL), :], e, es, my[pl.ds(row, SUBL), :], mm)
        py[pl.ds(row, SUBL), :] = qy
        xw = pltpu.roll(qx, 1, 1)
        yn = pltpu.roll(jnp.where(last_row, qy_above, qy), 1, 0)
        ph[pl.ds(row, SUBL), :] += RATE * (((xw - qx) + yn) - qy)
        return en, qy

    def step(n, _):
        e0 = ph[0:SUBL, :] + pz[0:SUBL, :]
        lax.fori_loop(0, chunks, chunk, (e0, jnp.zeros(full, jnp.float32)))
        return 0

    lax.fori_loop(0, STEPS, step, 0)

    def drain(i, _):
        row = pl.multiple_of(i * SUBL, SUBL)
        for f in range(3):
            v = packs[f][pl.ds(row + SUBL, SUBL), :]
            for q in range(count):
                at = q * pitch + HALO
                k, s = at // LANE, at % LANE
                lo = pltpu.roll(v[:, k * LANE : (k + 1) * LANE], LANE - s, 1)
                hi = pltpu.roll(v[:, (k + 1) * LANE : (k + 2) * LANE], LANE - s, 1)
                t = jnp.where(lane < LANE - s, lo, hi)
                if f > 0:
                    old = fields[f][rec(q, 0), pl.ds(row, SUBL), :]
                    t = jnp.where(rec(q, 1) == 1, t, old)
                if peers:
                    for o in range(peers):

                        @pl.when(rec(q, 26) == o + 1)
                        def _(o=o, q=q, t=t, f=f):
                            outs[o][f, rec(q, 27), pl.ds(row, SUBL), :] = t

                else:
                    outs[0][f, q, pl.ds(row, SUBL), :] = t
        return 0

    lax.fori_loop(0, nrow, drain, 0)


def final_kernel(tiles, peers, tbl, stay, *rest):
    got = rest[:peers]
    outs = rest[peers:]
    s = pl.program_id(0)
    off = tbl[tiles * REC + 2 * s]
    k = tbl[tiles * REC + 2 * s + 1]

    @pl.when(off == 0)
    def _():
        for f in range(3):
            outs[f][0] = stay[f, k]

    for o in range(peers):

        @pl.when(off == o + 1)
        def _(o=o):
            for f in range(3):
                outs[f][0] = got[o][f, k]


def shards(h, x, y, z, m, pb, pa, wet):
    tiles = h.shape[0]
    lanes = lax.axis_size(("col", "sub"))
    cols = lax.axis_size("col")
    rows = lax.axis_size("row")
    f32 = jnp.float32
    me = jnp.stack([lax.axis_index("row"), lax.axis_index(("col", "sub"))]).astype(jnp.int32)
    smem = pl.BlockSpec(memory_space=pltpu.SMEM)
    vmem = pl.BlockSpec(memory_space=pltpu.VMEM)
    total = pb.shape[0]
    words = tiles * REC + 2 * tiles
    peers = lanes - 1
    tbl = pl.pallas_call(
        functools.partial(table_kernel, tiles, lanes, rows),
        out_shape=jax.ShapeDtypeStruct((words,), jnp.int32),
        in_specs=[smem] * 4,
        out_specs=smem,
        scratch_shapes=[
            pltpu.SMEM((total,), jnp.int32),
            pltpu.SMEM((total,), jnp.int32),
            pltpu.SMEM((lanes,), jnp.int32),
        ],
        name="tables",
    )(me, pb, pa, wet)
    ring = jax.ShapeDtypeStruct((lanes, tiles, 5, SUBL, LANE), f32)
    gc, gu, gd = pl.pallas_call(
        functools.partial(halo_kernel, tiles),
        out_shape=(jax.ShapeDtypeStruct((lanes, tiles // 2, LANE, LANE), f32), ring, ring),
        in_specs=[vmem] * 5,
        out_specs=(vmem,) * 3,
        scratch_shapes=[
            pltpu.VMEM((tiles, 5, SUBL, LANE), f32),
            pltpu.VMEM((tiles, 5, SUBL, LANE), f32),
            pltpu.SemaphoreType.DMA((3, 2 * cols)),
            pltpu.SemaphoreType.DMA((3, lanes)),
            pltpu.SemaphoreType.DMA((2,)),
            pltpu.SemaphoreType.DMA((2,)),
        ],
        compiler_params=pltpu.CompilerParams(
            collective_id=0, has_side_effects=True, vmem_limit_bytes=VMEM_LIMIT
        ),
        name="halo",
    )(h, x, y, z, m)

    def run(first, count, npeers):
        width = -(-count * (LANE + 2 * HALO) // LANE) * LANE
        slots = PER_PEER if npeers else count
        shape = jax.ShapeDtypeStruct((3, slots, LANE, LANE), f32)
        nout = max(npeers, 1)
        big = pltpu.VMEM((LANE + 2 * SUBL, width), f32)
        return pl.pallas_call(
            functools.partial(steps_kernel, first, count, npeers),
            out_shape=(shape,) * nout,
            in_specs=[smem] + [vmem] * 8,
            out_specs=(vmem,) * nout,
            scratch_shapes=[big] * 7 + [pltpu.VMEM((3 * SUBL, width), f32)],
            compiler_params=pltpu.CompilerParams(vmem_limit_bytes=VMEM_LIMIT),
            cost_estimate=pl.CostEstimate(
                flops=count * LANE * LANE * STEPS * 400, bytes_accessed=8 << 20, transcendentals=0
            ),
            name="steps",
        )(tbl, h, x, y, z, m, gc, gu, gd)

    sent = run(0, MOVE, peers)
    got = [
        lax.ppermute(sent[o - 1], ("col", "sub"), [(i, (i + o) % lanes) for i in range(lanes)])
        for o in range(1, lanes)
    ]
    (stay,) = run(MOVE, tiles - MOVE, 0)
    slot = pl.BlockSpec((1, LANE, LANE), lambda s: (s, 0, 0))
    return pl.pallas_call(
        functools.partial(final_kernel, tiles, peers),
        grid=(tiles,),
        out_shape=(jax.ShapeDtypeStruct(h.shape, f32),) * 3,
        in_specs=[smem] + [vmem] * (1 + peers),
        out_specs=(slot,) * 3,
        compiler_params=pltpu.CompilerParams(vmem_limit_bytes=VMEM_LIMIT),
        name="final",
    )(tbl, stay, *got)


def solution(mesh):
    tile = P(("basin", "row", "col", "sub"), None, None)
    part = P("basin")
    return jax.shard_map(
        shards,
        mesh=mesh,
        in_specs=(tile,) * 5 + (part,) * 3,
        out_specs=(tile,) * 3,
        check_vma=False,
    )
```

time: 336 us -> 106 us (0.32)
  Pallas kernels: 0 us -> 96.8 us
  local copies, waits for them, and re-layouts: 91.3 us -> 5.87 us
  blocking collectives: 76 us -> 0 us
  starting transfers between devices: 70.6 us -> 1.58 us
  waiting for transfers between devices: 40.8 us -> 0.01 us
  other arithmetic: 39.1 us -> 0.59 us
  between operations: 15.1 us -> 0.71 us
    pallas_call x0 -> x5, Pallas kernels: none -> 96.8 us  [the longest x2 65.1 us: run(): pl.pallas_call(functools.partial(steps_kernel, first, count, npeers), out...]
    all_gather x13 -> x0, blocking collectives: 76 us -> none  [share_edges(): lax.all_gather(edge_rows[None], ('col', 'sub'), axis=1, tiled=True)]
    ppermute x26 -> x3, starting transfers between devices: 70.6 us -> 1.58 us  [shards(): lax.ppermute(sent[o - 1], ('col', 'sub'), [(i, (i + o) % lanes) for i in...]
    gather x59 -> x0, local copies, waits for them, and re-layouts: 45.3 us -> none  [the longest x1 4.77 us: shards(): chosen = block_piece[jnp.clip(position, 0, piece_rows - 1)]]
    all_gather x1 -> x0, waiting for transfers between devices: 34.1 us -> none  [shards(): lax.all_gather(stacked[chosen_slots], ('col', 'sub'), axis=0, tiled=True)]
    select_n x27 -> x0, other arithmetic: 27.5 us -> none  [the longest x6 20.1 us: shards(): flow_x = jnp.where(wet_cells, jnp.where(open_x, updated_x, 0.0), flow_x)]
    slice x35 -> x0, local copies, waits for them, and re-layouts: 21.7 us -> none  [the longest x6 8.08 us: shards(): surface[:, :, 1:]]
    add x18 -> x0, other arithmetic: 8.06 us -> none  [the longest x6 8 us: shards(): surface = depth_now + ground]
  transfers between devices with their start and end apart: 27 -> 3, of which waited for: 7 -> 0; matrix products, arithmetic and copies ran while one was open for 14% -> 0% of each run, Pallas kernels for 0% -> 25%
where the time goes in v1:
time: 106 us
  Pallas kernels  96.8 us (91%)
  local copies, waits for them, and re-layouts  5.87 us (6%)
  starting transfers between devices  1.58 us (1%)
    pallas_call x2, Pallas kernels, run(): pl.pallas_call(functools.partial(steps_kernel, first, count, npeers), out...  65.1 us
    pallas_call x1, Pallas kernels, shards(): pl.pallas_call(functools.partial(halo_kernel, tiles), out_shape=(jax.Shap...  23.3 us
    unnamed x14, local copies, waits for them, and re-layouts  5.87 us
    pallas_call x1, Pallas kernels, shards(): pl.pallas_call(functools.partial(table_kernel, tiles, lanes, rows), out_s...  4.89 us
    pallas_call x1, Pallas kernels, shards(): pl.pallas_call(functools.partial(final_kernel, tiles, peers), grid=(tiles...  3.52 us
  transfers between devices with their start and end apart: 3, of which 0 were waited for; matrix products, arithmetic and copies ran while one was open for 0% of the time, Pallas kernels for 25%

profile of v1, /device:TPU:9, one launch (start us, length us, event | category | flops | bytes accessed | tf_op | source)
XLA Modules:
  0.0 105.5 jit_solution(15163235314172102199)
XLA Ops:
  0.6 0.6 pad_add_fusion.me_ref
  1.2 4.9 %tables.1.tbl = s32[272]{0:T(512)} custom-call(s32[2]{0:T(128)} %pad_add_fusion.me_ref, s32[128]{0:T(128)} %pb_ref.1, s32[128]{0:T(128)} %pa_ref.1, s32[128]{0:T(128)} %wet_ref.1), custom_call_target="tpu_custom_call" | custom-call | tf_op jit(solution)/shard_map/tables/pallas_call | solution.py:448
  6.1 0.0 copy-start
  6.1 1.0 copy-done
  7.2 0.0 copy-start.2
  7.2 1.0 copy-done.2
  8.2 0.0 copy-start.3
  8.2 1.0 copy-done.3
  9.2 0.0 copy-start.4
  9.2 1.0 copy-done.4
  10.3 0.0 copy-start.5
  10.3 1.0 copy-done.5
  11.3 0.0 copy-start.1
  11.3 23.3 %halo.1 = (f32[4,4,128,128]{3,2,1,0:T(8,128)S(1)}, f32[4,8,5,8,128]{4,3,2,1,0:T(8,128)S(1)}, f32[4,8,5,8,128]{4,3,2,1,0:T(8,128)S(1)}) custom-call(f32[8,128,128]{2,1,0:T(8,128)S(1)} %copy-done, f32[8,128,128]{2,1,0:T(8,128)S(1)} %copy-done.2, f32[8,128,128]{2,1,0:T(8,128)S(1)} %copy-done.3, f32[8,128,128]{2,1,0:T(8,128)S(1)} %copy-done.4, ...), custom_call_target="tpu_custom_call" | custom-call | tf_op jit(solution)/shard_map/halo/pallas_call | solution.py:461
  34.6 0.0 copy-start.6
  34.6 0.0 copy-done.1
  34.6 0.7 copy-done.6
  35.3 38.6 %steps.3 = (f32[3,2,128,128]{3,2,1,0:T(8,128)S(1)}, f32[3,2,128,128]{3,2,1,0:T(8,128)S(1)}, f32[3,2,128,128]{3,2,1,0:T(8,128)S(1)}) custom-call(s32[272]{0:T(512)S(1)} %copy-done.6, f32[8,128,128]{2,1,0:T(8,128)S(1)} %copy-done.1, f32[8,128,128]{2,1,0:T(8,128)S(1)} %copy-done.2, f32[8,128,128]{2,1,0:T(8,128)S(1)} %copy-done.3, f32[8,128,128]{2,1,0:T(8,128)S(1)} %copy-done.4, ...), custom_call_target="tpu_custom_call" | custom-call | flops 157286400 | bytes 8388608 | tf_op jit(solution)/shard_map/steps/pallas_call | solution.py:486
  73.9 0.4 collective-permute-start
  74.3 1.2 %collective-permute-start.1 = (f32[3,2,128,128]{3,2,1,0:T(8,128)S(1)}, f32[3,2,128,128]{3,2,1,0:T(8,128)S(1)}, u32[]{:S(2)}, u32[]{:S(2)}) collective-permute-start(f32[3,2,128,128]{3,2,1,0:T(8,128)S(1)} %get-tuple-element.13), channel_id=1, source_target_pairs={{0,2},{1,3},{2,0},{3,1},{4,6},{5,7},{6,4},{7,5},{8,10},{9,11},{10,... | collective-permute-start | bytes 1179656 | tf_op jit(solution)/shard_map/ppermute | solution.py:501
  75.5 0.0 collective-permute-start.2
  75.5 26.5 %steps.2.stay = f32[3,4,128,128]{3,2,1,0:T(8,128)S(1)} custom-call(s32[272]{0:T(512)S(1)} %copy-done.6, f32[8,128,128]{2,1,0:T(8,128)S(1)} %copy-done.1, f32[8,128,128]{2,1,0:T(8,128)S(1)} %copy-done.2, f32[8,128,128]{2,1,0:T(8,128)S(1)} %copy-done.3, f32[8,128,128]{2,1,0:T(8,128)S(1)} %copy-done.4, f32[8,128,128]{2,1,0:T(8,128)S(1)} %copy-done.5, ...), custom_call_target="tpu_custom_call" | custom-call | flops 157286400 | bytes 8388608 | tf_op jit(solution)/shard_map/steps/pallas_call | solution.py:486
  102.0 0.0 collective-permute-done.rest_0_
  102.0 0.0 collective-permute-done.1.rest_1_
  102.0 0.0 collective-permute-done.2.rest_2_
  102.0 3.5 %final.1 = (f32[8,128,128]{2,1,0:T(8,128)}, f32[8,128,128]{2,1,0:T(8,128)}, f32[8,128,128]{2,1,0:T(8,128)}) custom-call(s32[272]{0:T(512)S(1)} %copy-done.6, f32[3,4,128,128]{3,2,1,0:T(8,128)S(1)} %steps.2.stay, f32[3,2,128,128]{3,2,1,0:T(8,128)S(1)} %collective-permute-done.rest_0_, f32[3,2,128,128]{3,2,1,0:T(8,128)S(1)} %collective-permute-done.1.rest_1_, ...), custom_call_target="tpu_custom_call" | custom-call | tf_op jit(solution)/shard_map/final/pallas_call | solution.py:506
Async XLA Ops:
  6.1 1.0 copy-start
  7.2 1.0 copy-start.2
  8.2 1.0 copy-start.3
  9.2 1.0 copy-start.4
  10.3 1.0 copy-start.5
  11.3 23.3 %copy-start.1 = (f32[8,128,128]{2,1,0:T(8,128)S(1)}, f32[8,128,128]{2,1,0:T(8,128)}, u32[]{:S(2)}) copy-start(f32[8,128,128]{2,1,0:T(8,128)} %h.5) | copy-start | bytes 1572868
  34.6 0.7 copy-start.6
  73.9 28.1 %collective-permute-start = (f32[3,2,128,128]{3,2,1,0:T(8,128)S(1)}, f32[3,2,128,128]{3,2,1,0:T(8,128)S(1)}, u32[]{:S(2)}, u32[]{:S(2)}) collective-permute-start(f32[3,2,128,128]{3,2,1,0:T(8,128)S(1)} %get-tuple-element.12), channel_id=1, source_target_pairs={{0,1},{1,2},{2,3},{3,0},{4,5},{5,6},{6,7},{7,4},{8,9},{9,10},{10,1... | collective-permute-start | bytes 1179656 | tf_op jit(solution)/shard_map/ppermute | solution.py:501
  74.3 27.7 %collective-permute-start.1 = (f32[3,2,128,128]{3,2,1,0:T(8,128)S(1)}, f32[3,2,128,128]{3,2,1,0:T(8,128)S(1)}, u32[]{:S(2)}, u32[]{:S(2)}) collective-permute-start(f32[3,2,128,128]{3,2,1,0:T(8,128)S(1)} %get-tuple-element.13), channel_id=1, source_target_pairs={{0,2},{1,3},{2,0},{3,1},{4,6},{5,7},{6,4},{7,5},{8,10},{9,11},{10,... | collective-permute-start | bytes 1179656 | tf_op jit(solution)/shard_map/ppermute | solution.py:501
  75.5 26.5 %collective-permute-start.2 = (f32[3,2,128,128]{3,2,1,0:T(8,128)S(1)}, f32[3,2,128,128]{3,2,1,0:T(8,128)S(1)}, u32[]{:S(2)}, u32[]{:S(2)}) collective-permute-start(f32[3,2,128,128]{3,2,1,0:T(8,128)S(1)} %get-tuple-element.14), channel_id=1, source_target_pairs={{0,3},{1,0},{2,1},{3,2},{4,7},{5,4},{6,5},{7,6},{8,11},{9,8},{10,9... | collective-permute-start | bytes 1179656 | tf_op jit(solution)/shard_map/ppermute | solution.py:501

commit v2 on v1

--- a/solution.py
+++ b/solution.py
@@ -1,4 +1,5 @@
 import functools
+import math
 import jax
 import jax.numpy as jnp
 from jax import lax
@@ -16,22 +17,36 @@
 RATE = 0.1
 DEPTH_FLOOR = 0.3
 CLOSED = 1e30
+POWER = -7.0 / 3.0 / math.log(2.0)
+UNROLL = 6
+FILL = 4
+READY = 3
+DRAIN = 4
 SUBL = 8
 LANE = 128
 SEG = 12
 HALF = 64
 REC = 32
+EDGE = 32
 MESH_ID = pl.DeviceIdType.MESH
 VMEM_LIMIT = 40 * 1024 * 1024
 
 DIRS = ((0, -1), (0, 1), (-1, 0), (-1, -1), (-1, 1), (1, 0), (1, -1), (1, 1))
 
 
-def table_kernel(tiles, lanes, rows, me_ref, pb_ref, pa_ref, wet_ref, tbl_ref, invb, inva, cnt):
+def split(v, n):
+    if n & (n - 1) == 0:
+        return v >> (n.bit_length() - 1), v & (n - 1)
+    return lax.div(v, n), lax.rem(v, n)
+
+
+def table_kernel(tiles, pb_ref, pa_ref, wet_ref, tbl_ref, invb, inva, cnt):
+    lanes = lax.axis_size("col") * lax.axis_size("sub")
+    rows = lax.axis_size("row")
     total = lanes * rows * tiles
     row_tiles = lanes * tiles
-    my_row = me_ref[0]
-    my_lane = me_ref[1]
+    my_row = lax.axis_index("row")
+    my_lane = lax.axis_index("col") * lax.axis_size("sub") + lax.axis_index("sub")
     my_dev = my_row * lanes + my_lane
 
     def fill(s, _):
@@ -39,30 +54,30 @@
         inva[pa_ref[s]] = s
         return 0
 
-    lax.fori_loop(0, total, fill, 0)
+    lax.fori_loop(0, total, fill, 0, unroll=16)
     for o in range(lanes):
         cnt[o] = 0
 
     def place(t, ranks):
         leave_rank, stay_rank = ranks
         tile = pb_ref[my_dev * tiles + t]
-        dest = inva[tile] // tiles
+        dest = split(inva[tile], tiles)[0]
         leaving = dest != my_dev
         pos = jnp.where(leaving, leave_rank, stay_rank)
         base = pos * REC
         tbl_ref[base] = t
         tbl_ref[base + 1] = wet_ref[tile]
-        trow = tile // row_tiles
-        tcol = tile % row_tiles
+        trow, tcol = split(tile, row_tiles)
         for d, (dr, dc) in enumerate(DIRS):
             r, c = trow + dr, tcol + dc
             exists = (r >= 0) & (r < rows) & (c >= 0) & (c < row_tiles)
             other = jnp.where(exists, r * row_tiles + c, 0)
-            where = invb[other] % row_tiles
+            ln, sl = split(split(invb[other], row_tiles)[1], tiles)
             tbl_ref[base + 2 + d] = jnp.where(exists, wet_ref[other], 0)
-            tbl_ref[base + 10 + 2 * d] = where // tiles
-            tbl_ref[base + 11 + 2 * d] = where % tiles
-        off = lax.rem(dest % lanes - my_lane + lanes, lanes)
+            tbl_ref[base + 10 + 2 * d] = ln
+            tbl_ref[base + 11 + 2 * d] = sl
+        off = split(dest, lanes)[1] - my_lane
+        off = jnp.where(off < 0, off + lanes, off)
         k = cnt[off]
         cnt[off] = k + 1
         tbl_ref[base + 26] = off
@@ -74,14 +89,13 @@
 
     def final(s, _):
         src = invb[pa_ref[my_dev * tiles + s]]
-        src_dev = src // tiles
-        off = lax.rem(my_lane - src_dev % lanes + lanes, lanes)
-
-        def rank(j, n):
-            same = (inva[pb_ref[src_dev * tiles + j]] // tiles == my_dev) & (j < src % tiles)
-            return n + same.astype(jnp.int32)
-
-        n = lax.fori_loop(0, tiles, rank, jnp.int32(0))
+        src_dev, src_slot = split(src, tiles)
+        off = my_lane - split(src_dev, lanes)[1]
+        off = jnp.where(off < 0, off + lanes, off)
+        n = jnp.int32(0)
+        for j in range(tiles):
+            same = (split(inva[pb_ref[src_dev * tiles + j]], tiles)[0] == my_dev) & (j < src_slot)
+            n = n + same.astype(jnp.int32)
         tbl_ref[tiles * REC + 2 * s] = off
         tbl_ref[tiles * REC + 2 * s + 1] = n
         return 0
@@ -89,7 +103,7 @@
     lax.fori_loop(0, tiles, final, 0)
 
 
-def halo_kernel(tiles, h, x, y, z, m, gc, gu, gd, top, bot, ssem, rsem, vs, vr):
+def halo_kernel(tiles, *refs):
     cols = lax.axis_size("col")
     rows = lax.axis_size("row")
     b = lax.axis_index("basin")
@@ -99,7 +113,7 @@
     other = 1 - s
     me = c * 2 + s
     sib = c * 2 + other
-    fields = (h, x, y, z, m)
+    fields, (gc, gu, gd, top, bot), (ssem, rsem, vs, vr) = refs[:5], refs[5:10], refs[10:]
 
     barrier = pltpu.get_barrier_semaphore()
     pl.semaphore_signal(barrier, inc=1, device_id=(b, r, c, other), device_id_type=MESH_ID)
@@ -116,9 +130,12 @@
     def _():
         pl.semaphore_signal(barrier, inc=1, device_id=(b, r + 1, c, s), device_id_type=MESH_ID)
 
-    for f in range(5):
-        top[:, f] = fields[f][:, 0:SUBL, :]
-        bot[:, f] = fields[f][:, LANE - SUBL : LANE, :]
+    for t in range(tiles):
+        first = [fields[f][t, 0:HALO, :] for f in range(5)]
+        last = [fields[f][t, LANE - HALO : LANE, :] for f in range(5)]
+        pad = [jnp.zeros((EDGE - 5 * HALO, LANE), jnp.float32)]
+        top[t] = jnp.concatenate(first + pad, axis=0)
+        bot[t] = jnp.concatenate(last + pad, axis=0)
 
     beside = jnp.where(r > 0, 1, 0) + jnp.where(r < rows - 1, 1, 0)
     pl.semaphore_wait(barrier, cols + beside)
@@ -156,7 +173,7 @@
         gc[me, blk, pl.ds(row, SUBL), :] = acc
         return 0
 
-    lax.fori_loop(0, (tiles // 2) * (LANE // SUBL), pack, 0)
+    lax.fori_loop(0, (tiles // 2) * (LANE // SUBL), pack, 0, unroll=4)
 
     bufs = (gc, gu, gd)
 
@@ -248,7 +265,7 @@
 
 def steps_kernel(first, count, peers, tbl, h, x, y, z, m, gc, gu, gd, *rest):
     outs = rest[: max(peers, 1)]
-    ph, px, py, pz, pm, mx, my, pw = rest[max(peers, 1) :]
+    ph, px, py, pz, pm, mx, my, pw, hold = rest[max(peers, 1) :]
     fields = (h, x, y, z, m)
     packs = (ph, px, py, pz, pm)
     width = ph.shape[1]
@@ -298,15 +315,16 @@
             save(packs[f], row + SUBL, acc)
         return 0
 
-    lax.fori_loop(0, nrow, fill, 0)
-    for row, buf, d0 in ((0, gu, 2), (LANE + SUBL, gd, 5)):
+    lax.fori_loop(0, nrow, fill, 0, unroll=FILL)
+    for row, buf, d0, lead in ((0, gu, 2, SUBL - HALO), (LANE + SUBL, gd, 5, 0)):
         for f in range(5):
             acc = fresh()
             for q in range(count):
                 at = q * pitch + HALO
                 got = []
                 for d in range(d0, d0 + 3):
-                    v = buf[rec(q, 10 + 2 * d), rec(q, 11 + 2 * d), f]
+                    v = buf[rec(q, 10 + 2 * d), rec(q, 11 + 2 * d)]
+                    v = pltpu.roll(v, (lead - f * HALO) % EDGE, 0)[0:SUBL]
                     got.append(jnp.where(rec(q, 2 + d) == 1, v, 0.0))
                 put(acc, got[0], 0, at, LANE)
                 put(acc, got[1], LANE - HALO, at - HALO, HALO)
@@ -354,13 +372,13 @@
         pm[pl.ds(row, SUBL), :] = (GRAV * STEP_TIME) * mm * mm
         return 0
 
-    lax.fori_loop(0, chunks, ready, 0)
+    lax.fori_loop(0, chunks, ready, 0, unroll=READY)
 
     def face(q, e, e2, mz, mm):
         f = jnp.maximum(e, e2) - mz
         num = q - (GRAV * STEP_TIME / SPACING) * jnp.maximum(f, 0.0) * (e2 - e)
-        g = jnp.exp((-7.0 / 3.0) * jnp.log(jnp.maximum(f, DEPTH_FLOOR)))
-        return num / (1.0 + mm * jnp.abs(q) * g)
+        g = jnp.exp2(POWER * jnp.log(jnp.maximum(f, DEPTH_FLOOR)))
+        return num, 1.0 + mm * jnp.abs(q) * g
 
     def chunk(i, carry):
         e, qy_above = carry
@@ -370,9 +388,11 @@
         mm = pm[pl.ds(row, SUBL), :]
         ee = pltpu.roll(e, width - 1, 1)
         es = pltpu.roll(jnp.where(first_row, en, e), SUBL - 1, 0)
-        qx = face(px[pl.ds(row, SUBL), :], e, ee, mx[pl.ds(row, SUBL), :], mm)
+        nx, rx = face(px[pl.ds(row, SUBL), :], e, ee, mx[pl.ds(row, SUBL), :], mm)
+        ny, ry = face(py[pl.ds(row, SUBL), :], e, es, my[pl.ds(row, SUBL), :], mm)
+        qx = nx / rx
+        qy = ny / ry
         px[pl.ds(row, SUBL), :] = qx
-        qy = face(py[pl.ds(row, SUBL), :], e, es, my[pl.ds(row, SUBL), :], mm)
         py[pl.ds(row, SUBL), :] = qy
         xw = pltpu.roll(qx, 1, 1)
         yn = pltpu.roll(jnp.where(last_row, qy_above, qy), 1, 0)
@@ -381,7 +401,7 @@
 
     def step(n, _):
         e0 = ph[0:SUBL, :] + pz[0:SUBL, :]
-        lax.fori_loop(0, chunks, chunk, (e0, jnp.zeros(full, jnp.float32)))
+        lax.fori_loop(0, chunks, chunk, (e0, jnp.zeros(full, jnp.float32)), unroll=UNROLL)
         return 0
 
     lax.fori_loop(0, STEPS, step, 0)
@@ -400,72 +420,73 @@
                     old = fields[f][rec(q, 0), pl.ds(row, SUBL), :]
                     t = jnp.where(rec(q, 1) == 1, t, old)
                 if peers:
-                    for o in range(peers):
-
-                        @pl.when(rec(q, 26) == o + 1)
-                        def _(o=o, q=q, t=t, f=f):
-                            outs[o][f, rec(q, 27), pl.ds(row, SUBL), :] = t
-
+                    slot = (rec(q, 26) - 1) * PER_PEER + rec(q, 27)
+                    hold[slot, f, pl.ds(row, SUBL), :] = t
                 else:
                     outs[0][f, q, pl.ds(row, SUBL), :] = t
         return 0
 
-    lax.fori_loop(0, nrow, drain, 0)
+    lax.fori_loop(0, nrow, drain, 0, unroll=DRAIN)
+    for o in range(peers):
+        for k in range(PER_PEER):
+            for f in range(3):
+                outs[o][f, k] = hold[o * PER_PEER + k, f]
 
 
 def final_kernel(tiles, peers, tbl, stay, *rest):
-    got = rest[:peers]
-    outs = rest[peers:]
-    s = pl.program_id(0)
-    off = tbl[tiles * REC + 2 * s]
-    k = tbl[tiles * REC + 2 * s + 1]
-
-    @pl.when(off == 0)
-    def _():
+    got, outs, sem = rest[:peers], rest[peers : peers + 3], rest[-1]
+
+    def send(ref, k, f, s):
+        return pltpu.make_async_copy(ref.at[f, k], outs[f].at[s], sem.at[f, s])
+
+    for s in range(tiles):
+        off = tbl[tiles * REC + 2 * s]
+        k = tbl[tiles * REC + 2 * s + 1]
+        for o, ref in enumerate((stay,) + got):
+
+            @pl.when(off == o)
+            def _(ref=ref, k=k, s=s):
+                for f in range(3):
+                    send(ref, k, f, s).start()
+
+    for s in range(tiles):
         for f in range(3):
-            outs[f][0] = stay[f, k]
-
-    for o in range(peers):
-
-        @pl.when(off == o + 1)
-        def _(o=o):
-            for f in range(3):
-                outs[f][0] = got[o][f, k]
+            send(stay, 0, f, s).wait()
 
 
 def shards(h, x, y, z, m, pb, pa, wet):
     tiles = h.shape[0]
     lanes = lax.axis_size(("col", "sub"))
     cols = lax.axis_size("col")
-    rows = lax.axis_size("row")
     f32 = jnp.float32
-    me = jnp.stack([lax.axis_index("row"), lax.axis_index(("col", "sub"))]).astype(jnp.int32)
     smem = pl.BlockSpec(memory_space=pltpu.SMEM)
     vmem = pl.BlockSpec(memory_space=pltpu.VMEM)
     total = pb.shape[0]
     words = tiles * REC + 2 * tiles
     peers = lanes - 1
     tbl = pl.pallas_call(
-        functools.partial(table_kernel, tiles, lanes, rows),
+        functools.partial(table_kernel, tiles),
         out_shape=jax.ShapeDtypeStruct((words,), jnp.int32),
-        in_specs=[smem] * 4,
+        in_specs=[smem] * 3,
         out_specs=smem,
         scratch_shapes=[
             pltpu.SMEM((total,), jnp.int32),
             pltpu.SMEM((total,), jnp.int32),
             pltpu.SMEM((lanes,), jnp.int32),
         ],
+        cost_estimate=pl.CostEstimate(
+            flops=0, bytes_accessed=16 << 20, transcendentals=0
+        ),
         name="tables",
-    )(me, pb, pa, wet)
-    ring = jax.ShapeDtypeStruct((lanes, tiles, 5, SUBL, LANE), f32)
+    )(pb, pa, wet)
+    ring = jax.ShapeDtypeStruct((lanes, tiles, EDGE, LANE), f32)
     gc, gu, gd = pl.pallas_call(
         functools.partial(halo_kernel, tiles),
         out_shape=(jax.ShapeDtypeStruct((lanes, tiles // 2, LANE, LANE), f32), ring, ring),
         in_specs=[vmem] * 5,
         out_specs=(vmem,) * 3,
-        scratch_shapes=[
-            pltpu.VMEM((tiles, 5, SUBL, LANE), f32),
-            pltpu.VMEM((tiles, 5, SUBL, LANE), f32),
+        scratch_shapes=[pltpu.VMEM((tiles, EDGE, LANE), f32)] * 2
+        + [
             pltpu.SemaphoreType.DMA((3, 2 * cols)),
             pltpu.SemaphoreType.DMA((3, lanes)),
             pltpu.SemaphoreType.DMA((2,)),
@@ -488,7 +509,11 @@
             out_shape=(shape,) * nout,
             in_specs=[smem] + [vmem] * 8,
             out_specs=(vmem,) * nout,
-            scratch_shapes=[big] * 7 + [pltpu.VMEM((3 * SUBL, width), f32)],
+            scratch_shapes=[big] * 7
+            + [
+                pltpu.VMEM((3 * SUBL, width), f32),
+                pltpu.VMEM((max(npeers, 1) * PER_PEER, 3, LANE, LANE), f32),
+            ],
             compiler_params=pltpu.CompilerParams(vmem_limit_bytes=VMEM_LIMIT),
             cost_estimate=pl.CostEstimate(
                 flops=count * LANE * LANE * STEPS * 400, bytes_accessed=8 << 20, transcendentals=0
@@ -502,13 +527,12 @@
         for o in range(1, lanes)
     ]
     (stay,) = run(MOVE, tiles - MOVE, 0)
-    slot = pl.BlockSpec((1, LANE, LANE), lambda s: (s, 0, 0))
     return pl.pallas_call(
         functools.partial(final_kernel, tiles, peers),
-        grid=(tiles,),
         out_shape=(jax.ShapeDtypeStruct(h.shape, f32),) * 3,
         in_specs=[smem] + [vmem] * (1 + peers),
-        out_specs=(slot,) * 3,
+        out_specs=(pl.BlockSpec(memory_space=pltpu.MemorySpace.HBM),) * 3,
+        scratch_shapes=[pltpu.SemaphoreType.DMA((3, tiles))],
         compiler_params=pltpu.CompilerParams(vmem_limit_bytes=VMEM_LIMIT),
         name="final",
     )(tbl, stay, *got)

time: 106 us -> 63.5 us (0.60)
  Pallas kernels: 96.8 us -> 51.5 us
  waiting for transfers between devices: 0.01 us -> 3.42 us
    pallas_call x2, Pallas kernels: 65.1 us -> 28.8 us  [run(): pl.pallas_call(functools.partial(steps_kernel, first, count, npeers), out...]
    pallas_call x1, Pallas kernels: 23.3 us -> 18.5 us  [shards(): pl.pallas_call(functools.partial(halo_kernel, tiles), out_shape=(jax.Shap...]
    pallas_call x2, Pallas kernels: 8.41 us -> 4.2 us  [the longest x1 2.31 us: shards(): pl.pallas_call(functools.partial(table_kernel, tiles), out_shape=jax.Shap...]
    ppermute x3, waiting for transfers between devices: 0.01 us -> 3.42 us  [shards(): lax.ppermute(sent[o - 1], ('col', 'sub'), [(i, (i + o) % lanes) for i in...]
  transfers between devices with their start and end apart: 3 -> 3, of which waited for: 0 -> 2; matrix products, arithmetic and copies ran while one was open for 0% -> 0% of each run, Pallas kernels for 25% -> 23%
where the time goes in v2:
time: 63.5 us; the launch traced here: 63.1 us
  Pallas kernels  51.5 us (81%)
  local copies, waits for them, and re-layouts  5.87 us (9%)
  waiting for transfers between devices  3.42 us (5%)
  starting transfers between devices  1.55 us (2%)
  between operations  0.7 us (1%)
    pallas_call x2, Pallas kernels, run(): pl.pallas_call(functools.partial(steps_kernel, first, count, npeers), out...  28.8 us
    pallas_call x1, Pallas kernels, shards(): pl.pallas_call(functools.partial(halo_kernel, tiles), out_shape=(jax.Shap...  18.5 us
    unnamed x14, local copies, waits for them, and re-layouts  5.87 us
    ppermute x3, waiting for transfers between devices, shards(): lax.ppermute(sent[o - 1], ('col', 'sub'), [(i, (i + o) % lanes) for i in...  3.42 us
    pallas_call x1, Pallas kernels, shards(): pl.pallas_call(functools.partial(table_kernel, tiles), out_shape=jax.Shap...  2.31 us
    pallas_call x1, Pallas kernels, shards(): pl.pallas_call(functools.partial(final_kernel, tiles, peers), out_shape=(...  1.9 us
    ppermute x3, starting transfers between devices, shards(): lax.ppermute(sent[o - 1], ('col', 'sub'), [(i, (i + o) % lanes) for i in...  1.55 us
  transfers between devices with their start and end apart: 3, of which 2 were waited for; matrix products, arithmetic and copies ran while one was open for 0% of the time, Pallas kernels for 23%

profile of v2, /device:TPU:9, one launch (start us, length us, event | category | flops | bytes accessed | tf_op | source)
XLA Modules:
  0.0 63.1 jit_solution(12617123275665529322)
XLA Ops:
  0.6 2.3 %tables.1.tbl = s32[272]{0:T(512)} custom-call(s32[128]{0:T(128)} %pb_ref.1, s32[128]{0:T(128)} %pa_ref.1, s32[128]{0:T(128)} %wet_ref.1), custom_call_target="tpu_custom_call" | custom-call | bytes 16777216 | tf_op jit(solution)/shard_map/tables/pallas_call | solution.py:467
  2.9 0.0 copy-start
  3.0 1.0 %copy-done = f32[8,128,128]{2,1,0:T(8,128)S(1)} copy-done((f32[8,128,128]{2,1,0:T(8,128)S(1)}, f32[8,128,128]{2,1,0:T(8,128)}, u32[]{:S(2)}) %copy-start) | copy-done | bytes 524312
  4.0 0.0 copy-start.2
  4.0 1.0 %copy-done.2 = f32[8,128,128]{2,1,0:T(8,128)S(1)} copy-done((f32[8,128,128]{2,1,0:T(8,128)S(1)}, f32[8,128,128]{2,1,0:T(8,128)}, u32[]{:S(2)}) %copy-start.2) | copy-done | bytes 524312
  5.0 0.0 copy-start.3
  5.0 1.0 %copy-done.3 = f32[8,128,128]{2,1,0:T(8,128)S(1)} copy-done((f32[8,128,128]{2,1,0:T(8,128)S(1)}, f32[8,128,128]{2,1,0:T(8,128)}, u32[]{:S(2)}) %copy-start.3) | copy-done | bytes 524312
  6.1 0.0 copy-start.4
  6.1 1.0 %copy-done.4 = f32[8,128,128]{2,1,0:T(8,128)S(1)} copy-done((f32[8,128,128]{2,1,0:T(8,128)S(1)}, f32[8,128,128]{2,1,0:T(8,128)}, u32[]{:S(2)}) %copy-start.4) | copy-done | bytes 524312
  7.1 0.0 copy-start.5
  7.1 1.0 %copy-done.5 = f32[8,128,128]{2,1,0:T(8,128)S(1)} copy-done((f32[8,128,128]{2,1,0:T(8,128)S(1)}, f32[8,128,128]{2,1,0:T(8,128)}, u32[]{:S(2)}) %copy-start.5) | copy-done | bytes 524312
  8.2 0.0 copy-start.1
  8.2 18.5 %halo.1 = (f32[4,4,128,128]{3,2,1,0:T(8,128)S(1)}, f32[4,8,32,128]{3,2,1,0:T(8,128)S(1)}, f32[4,8,32,128]{3,2,1,0:T(8,128)S(1)}) custom-call(f32[8,128,128]{2,1,0:T(8,128)S(1)} %copy-done, f32[8,128,128]{2,1,0:T(8,128)S(1)} %copy-done.2, f32[8,128,128]{2,1,0:T(8,128)S(1)} %copy-done.3, f32[8,128,128]{2,1,0:T(8,128)S(1)} %copy-done.4, ...), custom_call_target="tpu_custom_call" | custom-call | tf_op jit(solution)/shard_map/halo/pallas_call | solution.py:483
  26.7 0.0 copy-start.6
  26.7 0.0 copy-done.1
  26.7 0.7 %copy-done.6 = s32[272]{0:T(512)S(1)} copy-done((s32[272]{0:T(512)S(1)}, s32[272]{0:T(512)}, u32[]{:S(2)}) %copy-start.6) | copy-done | bytes 1112
  27.4 14.4 %steps.3 = (f32[3,2,128,128]{3,2,1,0:T(8,128)S(1)}, f32[3,2,128,128]{3,2,1,0:T(8,128)S(1)}, f32[3,2,128,128]{3,2,1,0:T(8,128)S(1)}) custom-call(s32[272]{0:T(512)S(1)} %copy-done.6, f32[8,128,128]{2,1,0:T(8,128)S(1)} %copy-done.1, f32[8,128,128]{2,1,0:T(8,128)S(1)} %copy-done.2, f32[8,128,128]{2,1,0:T(8,128)S(1)} %copy-done.3, f32[8,128,128]{2,1,0:T(8,128)S(1)} %copy-done.4, ...), custom_call_target="tpu_custom_call" | custom-call | flops 157286400 | bytes 8388608 | tf_op jit(solution)/shard_map/steps/pallas_call | solution.py:507
  41.8 0.3 collective-permute-start
  42.1 1.2 %collective-permute-start.1 = (f32[3,2,128,128]{3,2,1,0:T(8,128)S(1)}, f32[3,2,128,128]{3,2,1,0:T(8,128)S(1)}, u32[]{:S(2)}, u32[]{:S(2)}) collective-permute-start(f32[3,2,128,128]{3,2,1,0:T(8,128)S(1)} %get-tuple-element.13), channel_id=1, source_target_pairs={{0,2},{1,3},{2,0},{3,1},{4,6},{5,7},{6,4},{7,5},{8,10},{9,11},{10,... | collective-permute-start | bytes 1179656 | tf_op jit(solution)/shard_map/ppermute | solution.py:526
  43.4 0.0 collective-permute-start.2
  43.4 14.4 %steps.2.stay = f32[3,4,128,128]{3,2,1,0:T(8,128)S(1)} custom-call(s32[272]{0:T(512)S(1)} %copy-done.6, f32[8,128,128]{2,1,0:T(8,128)S(1)} %copy-done.1, f32[8,128,128]{2,1,0:T(8,128)S(1)} %copy-done.2, f32[8,128,128]{2,1,0:T(8,128)S(1)} %copy-done.3, f32[8,128,128]{2,1,0:T(8,128)S(1)} %copy-done.4, f32[8,128,128]{2,1,0:T(8,128)S(1)} %copy-done.5, ...), custom_call_target="tpu_custom_call" | custom-call | flops 157286400 | bytes 8388608 | tf_op jit(solution)/shard_map/steps/pallas_call | solution.py:507
  57.7 0.0 collective-permute-done.rest_0_
  57.7 2.5 %collective-permute-done.1.rest_1_ = f32[3,2,128,128]{3,2,1,0:T(8,128)S(1)} collective-permute-done((f32[3,2,128,128]{3,2,1,0:T(8,128)S(1)}, f32[3,2,128,128]{3,2,1,0:T(8,128)S(1)}, u32[]{:S(2)}, u32[]{:S(2)}) %collective-permute-start.1) | collective-permute-done | bytes 393248 | tf_op jit(solution)/shard_map/ppermute | solution.py:526
  60.2 0.9 %collective-permute-done.2.rest_2_ = f32[3,2,128,128]{3,2,1,0:T(8,128)S(1)} collective-permute-done((f32[3,2,128,128]{3,2,1,0:T(8,128)S(1)}, f32[3,2,128,128]{3,2,1,0:T(8,128)S(1)}, u32[]{:S(2)}, u32[]{:S(2)}) %collective-permute-start.2) | collective-permute-done | bytes 393248 | tf_op jit(solution)/shard_map/ppermute | solution.py:526
  61.2 1.9 %final.1 = (f32[8,128,128]{2,1,0:T(8,128)}, f32[8,128,128]{2,1,0:T(8,128)}, f32[8,128,128]{2,1,0:T(8,128)}) custom-call(s32[272]{0:T(512)S(1)} %copy-done.6, f32[3,4,128,128]{3,2,1,0:T(8,128)S(1)} %steps.2.stay, f32[3,2,128,128]{3,2,1,0:T(8,128)S(1)} %collective-permute-done.rest_0_, f32[3,2,128,128]{3,2,1,0:T(8,128)S(1)} %collective-permute-done.1.rest_1_, ...), custom_call_target="tpu_custom_call" | custom-call | tf_op jit(solution)/shard_map/final/pallas_call | solution.py:530
Async XLA Ops:
  2.9 1.0 %copy-start = (f32[8,128,128]{2,1,0:T(8,128)S(1)}, f32[8,128,128]{2,1,0:T(8,128)}, u32[]{:S(2)}) copy-start(f32[8,128,128]{2,1,0:T(8,128)} %h.3) | copy-start | bytes 1572868
  4.0 1.0 %copy-start.2 = (f32[8,128,128]{2,1,0:T(8,128)S(1)}, f32[8,128,128]{2,1,0:T(8,128)}, u32[]{:S(2)}) copy-start(f32[8,128,128]{2,1,0:T(8,128)} %x.3) | copy-start | bytes 1572868
  5.0 1.0 %copy-start.3 = (f32[8,128,128]{2,1,0:T(8,128)S(1)}, f32[8,128,128]{2,1,0:T(8,128)}, u32[]{:S(2)}) copy-start(f32[8,128,128]{2,1,0:T(8,128)} %y.3) | copy-start | bytes 1572868
  6.1 1.0 %copy-start.4 = (f32[8,128,128]{2,1,0:T(8,128)S(1)}, f32[8,128,128]{2,1,0:T(8,128)}, u32[]{:S(2)}) copy-start(f32[8,128,128]{2,1,0:T(8,128)} %z.3) | copy-start | bytes 1572868
  7.1 1.0 %copy-start.5 = (f32[8,128,128]{2,1,0:T(8,128)S(1)}, f32[8,128,128]{2,1,0:T(8,128)}, u32[]{:S(2)}) copy-start(f32[8,128,128]{2,1,0:T(8,128)} %m.3) | copy-start | bytes 1572868
  8.2 18.5 %copy-start.1 = (f32[8,128,128]{2,1,0:T(8,128)S(1)}, f32[8,128,128]{2,1,0:T(8,128)}, u32[]{:S(2)}) copy-start(f32[8,128,128]{2,1,0:T(8,128)} %h.3) | copy-start | bytes 1572868
  26.7 0.7 %copy-start.6 = (s32[272]{0:T(512)S(1)}, s32[272]{0:T(512)}, u32[]{:S(2)}) copy-start(s32[272]{0:T(512)} %tables.1.tbl) | copy-start | bytes 3268
  41.8 15.9 %collective-permute-start = (f32[3,2,128,128]{3,2,1,0:T(8,128)S(1)}, f32[3,2,128,128]{3,2,1,0:T(8,128)S(1)}, u32[]{:S(2)}, u32[]{:S(2)}) collective-permute-start(f32[3,2,128,128]{3,2,1,0:T(8,128)S(1)} %get-tuple-element.12), channel_id=1, source_target_pairs={{0,1},{1,2},{2,3},{3,0},{4,5},{5,6},{6,7},{7,4},{8,9},{9,10},{10,1... | collective-permute-start | bytes 1179656 | tf_op jit(solution)/shard_map/ppermute | solution.py:526
  42.1 18.1 %collective-permute-start.1 = (f32[3,2,128,128]{3,2,1,0:T(8,128)S(1)}, f32[3,2,128,128]{3,2,1,0:T(8,128)S(1)}, u32[]{:S(2)}, u32[]{:S(2)}) collective-permute-start(f32[3,2,128,128]{3,2,1,0:T(8,128)S(1)} %get-tuple-element.13), channel_id=1, source_target_pairs={{0,2},{1,3},{2,0},{3,1},{4,6},{5,7},{6,4},{7,5},{8,10},{9,11},{10,... | collective-permute-start | bytes 1179656 | tf_op jit(solution)/shard_map/ppermute | solution.py:526
  43.4 17.8 %collective-permute-start.2 = (f32[3,2,128,128]{3,2,1,0:T(8,128)S(1)}, f32[3,2,128,128]{3,2,1,0:T(8,128)S(1)}, u32[]{:S(2)}, u32[]{:S(2)}) collective-permute-start(f32[3,2,128,128]{3,2,1,0:T(8,128)S(1)} %get-tuple-element.14), channel_id=1, source_target_pairs={{0,3},{1,0},{2,1},{3,2},{4,7},{5,4},{6,5},{7,6},{8,11},{9,8},{10,9... | collective-permute-start | bytes 1179656 | tf_op jit(solution)/shard_map/ppermute | solution.py:526

commit v3 on v2

--- a/solution.py
+++ b/solution.py
@@ -18,10 +18,10 @@
 DEPTH_FLOOR = 0.3
 CLOSED = 1e30
 POWER = -7.0 / 3.0 / math.log(2.0)
-UNROLL = 6
-FILL = 4
-READY = 3
-DRAIN = 4
+UNROLL = 18
+FILL = 16
+READY = 18
+DRAIN = 16
 SUBL = 8
 LANE = 128
 SEG = 12
@@ -475,7 +475,7 @@
             pltpu.SMEM((lanes,), jnp.int32),
         ],
         cost_estimate=pl.CostEstimate(
-            flops=0, bytes_accessed=16 << 20, transcendentals=0
+            flops=4_000_000_000, bytes_accessed=16 << 20, transcendentals=0
         ),
         name="tables",
     )(pb, pa, wet)

time: 63.5 us -> 51.3 us (0.81)
  Pallas kernels: 51.5 us -> 37.6 us
  waiting for transfers between devices: 3.42 us -> 10.5 us
  local copies, waits for them, and re-layouts: 5.87 us -> 0.7 us
    pallas_call x2, Pallas kernels: 28.8 us -> 14.7 us  [run(): pl.pallas_call(functools.partial(steps_kernel, first, count, npeers), out...]
    ppermute x3, waiting for transfers between devices: 3.42 us -> 10.5 us  [shards(): lax.ppermute(sent[o - 1], ('col', 'sub'), [(i, (i + o) % lanes) for i in...]
    unnamed x14 -> x12, local copies, waits for them, and re-layouts: 5.87 us -> 0.7 us
  transfers between devices with their start and end apart: 3 -> 3, of which waited for: 2 -> 2; matrix products, arithmetic and copies ran while one was open for 0% -> 0% of each run, Pallas kernels for 23% -> 14%
where the time goes in v3:
time: 51.3 us; the launch traced here: 51.1 us
  Pallas kernels  37.6 us (73%)
  waiting for transfers between devices  10.5 us (20%)
  starting transfers between devices  1.55 us (3%)
  between operations  0.76 us (1%)
  local copies, waits for them, and re-layouts  0.7 us (1%)
    pallas_call x1, Pallas kernels, shards(): pl.pallas_call(functools.partial(halo_kernel, tiles), out_shape=(jax.Shap...  18.6 us
    pallas_call x2, Pallas kernels, run(): pl.pallas_call(functools.partial(steps_kernel, first, count, npeers), out...  14.7 us
    ppermute x3, waiting for transfers between devices, shards(): lax.ppermute(sent[o - 1], ('col', 'sub'), [(i, (i + o) % lanes) for i in...  10.5 us
    pallas_call x1, Pallas kernels, shards(): pl.pallas_call(functools.partial(table_kernel, tiles), out_shape=jax.Shap...  2.44 us
    pallas_call x1, Pallas kernels, shards(): pl.pallas_call(functools.partial(final_kernel, tiles, peers), out_shape=(...  1.89 us
    ppermute x3, starting transfers between devices, shards(): lax.ppermute(sent[o - 1], ('col', 'sub'), [(i, (i + o) % lanes) for i in...  1.55 us
  transfers between devices with their start and end apart: 3, of which 2 were waited for; matrix products, arithmetic and copies ran while one was open for 0% of the time, Pallas kernels for 14%

profile of v3, /device:TPU:9, one launch (start us, length us, event | category | flops | bytes accessed | tf_op | source)
XLA Modules:
  0.0 51.1 jit_solution(14629984809504184735)
XLA Ops:
  0.6 0.0 copy-start.2
  0.6 0.0 copy-start.3
  0.7 0.0 copy-start.4
  0.7 0.0 copy-start
  0.7 0.0 copy-start.1
  0.7 2.4 %tables.1.tbl = s32[272]{0:T(512)} custom-call(s32[128]{0:T(128)} %pb_ref.1, s32[128]{0:T(128)} %pa_ref.1, s32[128]{0:T(128)} %wet_ref.1), custom_call_target="tpu_custom_call" | custom-call | flops 4000000000 | bytes 16777216 | tf_op jit(solution)/shard_map/tables/pallas_call | solution.py:467
  3.1 0.0 copy-done.2
  3.1 0.0 copy-done.3
  3.2 0.0 copy-done.4
  3.2 0.0 copy-done
  3.2 0.0 copy-done.1
  3.2 18.6 %halo.1 = (f32[4,4,128,128]{3,2,1,0:T(8,128)S(1)}, f32[4,8,32,128]{3,2,1,0:T(8,128)S(1)}, f32[4,8,32,128]{3,2,1,0:T(8,128)S(1)}) custom-call(f32[8,128,128]{2,1,0:T(8,128)S(1)} %copy-done, f32[8,128,128]{2,1,0:T(8,128)S(1)} %copy-done.1, f32[8,128,128]{2,1,0:T(8,128)S(1)} %copy-done.2, f32[8,128,128]{2,1,0:T(8,128)S(1)} %copy-done.3, ...), custom_call_target="tpu_custom_call" | custom-call | tf_op jit(solution)/shard_map/halo/pallas_call | solution.py:483
  21.8 0.0 copy-start.5
  21.8 0.7 %copy-done.5 = s32[272]{0:T(512)S(1)} copy-done((s32[272]{0:T(512)S(1)}, s32[272]{0:T(512)}, u32[]{:S(2)}) %copy-start.5) | copy-done | bytes 1112
  22.4 7.4 %steps.3 = (f32[3,2,128,128]{3,2,1,0:T(8,128)S(1)}, f32[3,2,128,128]{3,2,1,0:T(8,128)S(1)}, f32[3,2,128,128]{3,2,1,0:T(8,128)S(1)}) custom-call(s32[272]{0:T(512)S(1)} %copy-done.5, f32[8,128,128]{2,1,0:T(8,128)S(1)} %copy-done, f32[8,128,128]{2,1,0:T(8,128)S(1)} %copy-done.1, f32[8,128,128]{2,1,0:T(8,128)S(1)} %copy-done.2, f32[8,128,128]{2,1,0:T(8,128)S(1)} %copy-done.3, ...), custom_call_target="tpu_custom_call" | custom-call | flops 157286400 | bytes 8388608 | tf_op jit(solution)/shard_map/steps/pallas_call | solution.py:507
  29.8 0.3 collective-permute-start
  30.2 1.2 %collective-permute-start.1 = (f32[3,2,128,128]{3,2,1,0:T(8,128)S(1)}, f32[3,2,128,128]{3,2,1,0:T(8,128)S(1)}, u32[]{:S(2)}, u32[]{:S(2)}) collective-permute-start(f32[3,2,128,128]{3,2,1,0:T(8,128)S(1)} %get-tuple-element.13), channel_id=1, source_target_pairs={{0,2},{1,3},{2,0},{3,1},{4,6},{5,7},{6,4},{7,5},{8,10},{9,11},{10,... | collective-permute-start | bytes 1179656 | tf_op jit(solution)/shard_map/ppermute | solution.py:526
  31.4 0.0 collective-permute-start.2
  31.4 7.3 %steps.2.stay = f32[3,4,128,128]{3,2,1,0:T(8,128)S(1)} custom-call(s32[272]{0:T(512)S(1)} %copy-done.5, f32[8,128,128]{2,1,0:T(8,128)S(1)} %copy-done, f32[8,128,128]{2,1,0:T(8,128)S(1)} %copy-done.1, f32[8,128,128]{2,1,0:T(8,128)S(1)} %copy-done.2, f32[8,128,128]{2,1,0:T(8,128)S(1)} %copy-done.3, f32[8,128,128]{2,1,0:T(8,128)S(1)} %copy-done.4, ...), custom_call_target="tpu_custom_call" | custom-call | flops 157286400 | bytes 8388608 | tf_op jit(solution)/shard_map/steps/pallas_call | solution.py:507
  38.7 0.0 collective-permute-done.rest_0_
  38.7 9.5 %collective-permute-done.1.rest_1_ = f32[3,2,128,128]{3,2,1,0:T(8,128)S(1)} collective-permute-done((f32[3,2,128,128]{3,2,1,0:T(8,128)S(1)}, f32[3,2,128,128]{3,2,1,0:T(8,128)S(1)}, u32[]{:S(2)}, u32[]{:S(2)}) %collective-permute-start.1) | collective-permute-done | bytes 393248 | tf_op jit(solution)/shard_map/ppermute | solution.py:526
  48.2 0.9 %collective-permute-done.2.rest_2_ = f32[3,2,128,128]{3,2,1,0:T(8,128)S(1)} collective-permute-done((f32[3,2,128,128]{3,2,1,0:T(8,128)S(1)}, f32[3,2,128,128]{3,2,1,0:T(8,128)S(1)}, u32[]{:S(2)}, u32[]{:S(2)}) %collective-permute-start.2) | collective-permute-done | bytes 393248 | tf_op jit(solution)/shard_map/ppermute | solution.py:526
  49.2 1.9 %final.1 = (f32[8,128,128]{2,1,0:T(8,128)}, f32[8,128,128]{2,1,0:T(8,128)}, f32[8,128,128]{2,1,0:T(8,128)}) custom-call(s32[272]{0:T(512)S(1)} %copy-done.5, f32[3,4,128,128]{3,2,1,0:T(8,128)S(1)} %steps.2.stay, f32[3,2,128,128]{3,2,1,0:T(8,128)S(1)} %collective-permute-done.rest_0_, f32[3,2,128,128]{3,2,1,0:T(8,128)S(1)} %collective-permute-done.1.rest_1_, ...), custom_call_target="tpu_custom_call" | custom-call | tf_op jit(solution)/shard_map/final/pallas_call | solution.py:530
Async XLA Ops:
  0.6 2.5 %copy-start.2 = (f32[8,128,128]{2,1,0:T(8,128)S(1)}, f32[8,128,128]{2,1,0:T(8,128)}, u32[]{:S(2)}) copy-start(f32[8,128,128]{2,1,0:T(8,128)} %y.3) | copy-start | bytes 1572868
  0.6 2.5 %copy-start.3 = (f32[8,128,128]{2,1,0:T(8,128)S(1)}, f32[8,128,128]{2,1,0:T(8,128)}, u32[]{:S(2)}) copy-start(f32[8,128,128]{2,1,0:T(8,128)} %z.3) | copy-start | bytes 1572868
  0.7 2.5 %copy-start.4 = (f32[8,128,128]{2,1,0:T(8,128)S(1)}, f32[8,128,128]{2,1,0:T(8,128)}, u32[]{:S(2)}) copy-start(f32[8,128,128]{2,1,0:T(8,128)} %m.3) | copy-start | bytes 1572868
  0.7 2.5 %copy-start = (f32[8,128,128]{2,1,0:T(8,128)S(1)}, f32[8,128,128]{2,1,0:T(8,128)}, u32[]{:S(2)}) copy-start(f32[8,128,128]{2,1,0:T(8,128)} %h.3) | copy-start | bytes 1572868
  0.7 2.5 %copy-start.1 = (f32[8,128,128]{2,1,0:T(8,128)S(1)}, f32[8,128,128]{2,1,0:T(8,128)}, u32[]{:S(2)}) copy-start(f32[8,128,128]{2,1,0:T(8,128)} %x.3) | copy-start | bytes 1572868
  21.8 0.7 %copy-start.5 = (s32[272]{0:T(512)S(1)}, s32[272]{0:T(512)}, u32[]{:S(2)}) copy-start(s32[272]{0:T(512)} %tables.1.tbl) | copy-start | bytes 3268
  29.8 8.9 %collective-permute-start = (f32[3,2,128,128]{3,2,1,0:T(8,128)S(1)}, f32[3,2,128,128]{3,2,1,0:T(8,128)S(1)}, u32[]{:S(2)}, u32[]{:S(2)}) collective-permute-start(f32[3,2,128,128]{3,2,1,0:T(8,128)S(1)} %get-tuple-element.12), channel_id=1, source_target_pairs={{0,1},{1,2},{2,3},{3,0},{4,5},{5,6},{6,7},{7,4},{8,9},{9,10},{10,1... | collective-permute-start | bytes 1179656 | tf_op jit(solution)/shard_map/ppermute | solution.py:526
  30.2 18.1 %collective-permute-start.1 = (f32[3,2,128,128]{3,2,1,0:T(8,128)S(1)}, f32[3,2,128,128]{3,2,1,0:T(8,128)S(1)}, u32[]{:S(2)}, u32[]{:S(2)}) collective-permute-start(f32[3,2,128,128]{3,2,1,0:T(8,128)S(1)} %get-tuple-element.13), channel_id=1, source_target_pairs={{0,2},{1,3},{2,0},{3,1},{4,6},{5,7},{6,4},{7,5},{8,10},{9,11},{10,... | collective-permute-start | bytes 1179656 | tf_op jit(solution)/shard_map/ppermute | solution.py:526
  31.4 17.8 %collective-permute-start.2 = (f32[3,2,128,128]{3,2,1,0:T(8,128)S(1)}, f32[3,2,128,128]{3,2,1,0:T(8,128)S(1)}, u32[]{:S(2)}, u32[]{:S(2)}) collective-permute-start(f32[3,2,128,128]{3,2,1,0:T(8,128)S(1)} %get-tuple-element.14), channel_id=1, source_target_pairs={{0,3},{1,0},{2,1},{3,2},{4,7},{5,4},{6,5},{7,6},{8,11},{9,8},{10,9... | collective-permute-start | bytes 1179656 | tf_op jit(solution)/shard_map/ppermute | solution.py:526

commit v4 on v3

--- a/solution.py
+++ b/solution.py
@@ -160,27 +160,26 @@
 
     lane = lax.broadcasted_iota(jnp.int32, (SUBL, LANE), 1)
 
-    def pack(i, _):
-        blk = i // (LANE // SUBL)
-        row = pl.multiple_of((i % (LANE // SUBL)) * SUBL, SUBL)
-        acc = jnp.zeros((SUBL, LANE), jnp.float32)
-        for u in range(2):
-            for f in range(5):
-                base = u * HALF + f * SEG
-                v = fields[f][2 * blk + u, pl.ds(row, SUBL), :]
-                v = pltpu.roll(v, (base - (LANE - HALO)) % LANE, 1)
-                acc = jnp.where((lane >= base) & (lane < base + SEG), v, acc)
-        gc[me, blk, pl.ds(row, SUBL), :] = acc
-        return 0
-
-    lax.fori_loop(0, (tiles // 2) * (LANE // SUBL), pack, 0, unroll=4)
-
-    bufs = (gc, gu, gd)
+    def pack(blk):
+        for row in range(0, LANE, SUBL):
+            acc = jnp.zeros((SUBL, LANE), jnp.float32)
+            for u in range(2):
+                for f in range(5):
+                    base = u * HALF + f * SEG
+                    v = fields[f][2 * blk + u, row : row + SUBL, :]
+                    v = pltpu.roll(v, (base - (LANE - HALO)) % LANE, 1)
+                    acc = jnp.where((lane >= base) & (lane < base + SEG), v, acc)
+            gc[me, blk, row : row + SUBL, :] = acc
+
+    blocks = tiles // 2
+
+    def part(kind, slot):
+        return gc.at[slot, kind] if kind < blocks else (gu, gd)[kind - blocks].at[slot]
 
     def across(kind, d):
         return pltpu.make_async_remote_copy(
-            bufs[kind].at[me],
-            bufs[kind].at[me],
+            part(kind, me),
+            part(kind, me),
             ssem.at[kind, d],
             rsem.at[kind, me],
             device_id=(b, r, lax.rem(c + d, cols), s),
@@ -190,8 +189,8 @@
     def sideways(kind, src_col, d):
         slot = src_col * 2 + s
         return pltpu.make_async_remote_copy(
-            bufs[kind].at[slot],
-            bufs[kind].at[slot],
+            part(kind, slot),
+            part(kind, slot),
             ssem.at[kind, cols + d],
             rsem.at[kind, slot],
             device_id=(b, r, c, other),
@@ -200,8 +199,8 @@
 
     def arrived(kind, slot):
         pltpu.make_async_remote_copy(
-            bufs[kind].at[slot],
-            bufs[kind].at[slot],
+            part(kind, slot),
+            part(kind, slot),
             ssem.at[kind, 0],
             rsem.at[kind, slot],
             device_id=(b, r, c, other),
@@ -228,38 +227,42 @@
         for d in range(cols):
             sideways(kind, lax.rem(c + d, cols), d).wait_send()
 
-    spread(0)
+    for blk in range(blocks):
+        pack(blk)
+        spread(blk)
 
     @pl.when(r < rows - 1)
     def _():
         up_copy().wait_recv()
-        spread(2)
+        spread(blocks + 1)
 
     @pl.when(r > 0)
     def _():
         down_copy().wait_recv()
-        spread(1)
-
-    relay(0)
+        spread(blocks)
+
+    for blk in range(blocks):
+        relay(blk)
 
     @pl.when(r < rows - 1)
     def _():
-        relay(2)
+        relay(blocks + 1)
 
     @pl.when(r > 0)
     def _():
-        relay(1)
-
-    close(0)
+        relay(blocks)
+
+    for blk in range(blocks):
+        close(blk)
 
     @pl.when(r < rows - 1)
     def _():
-        close(2)
+        close(blocks + 1)
         down_copy().wait_send()
 
     @pl.when(r > 0)
     def _():
-        close(1)
+        close(blocks)
         up_copy().wait_send()
 
 
@@ -487,8 +490,8 @@
         out_specs=(vmem,) * 3,
         scratch_shapes=[pltpu.VMEM((tiles, EDGE, LANE), f32)] * 2
         + [
-            pltpu.SemaphoreType.DMA((3, 2 * cols)),
-            pltpu.SemaphoreType.DMA((3, lanes)),
+            pltpu.SemaphoreType.DMA((tiles // 2 + 2, 2 * cols)),
+            pltpu.SemaphoreType.DMA((tiles // 2 + 2, lanes)),
             pltpu.SemaphoreType.DMA((2,)),
             pltpu.SemaphoreType.DMA((2,)),
         ],

time: 51.3 us -> 49.7 us (0.969)
  Pallas kernels: 37.6 us -> 36 us
    pallas_call x1, Pallas kernels: 18.6 us -> 17 us  [shards(): pl.pallas_call(functools.partial(halo_kernel, tiles), out_shape=(jax.Shap...]
  transfers between devices with their start and end apart: 3 -> 3, of which waited for: 2 -> 2; matrix products, arithmetic and copies ran while one was open for 0% -> 0% of each run, Pallas kernels for 14% -> 15%
where the time goes in v4:
time: 49.7 us; the launch traced here: 49.5 us
  Pallas kernels  36 us (72%)
  waiting for transfers between devices  10.5 us (21%)
  starting transfers between devices  1.55 us (3%)
  between operations  0.76 us (2%)
  local copies, waits for them, and re-layouts  0.7 us (1%)
    pallas_call x1, Pallas kernels, shards(): pl.pallas_call(functools.partial(halo_kernel, tiles), out_shape=(jax.Shap...  17 us
    pallas_call x2, Pallas kernels, run(): pl.pallas_call(functools.partial(steps_kernel, first, count, npeers), out...  14.7 us
    ppermute x3, waiting for transfers between devices, shards(): lax.ppermute(sent[o - 1], ('col', 'sub'), [(i, (i + o) % lanes) for i in...  10.5 us
    pallas_call x1, Pallas kernels, shards(): pl.pallas_call(functools.partial(table_kernel, tiles), out_shape=jax.Shap...  2.44 us
    pallas_call x1, Pallas kernels, shards(): pl.pallas_call(functools.partial(final_kernel, tiles, peers), out_shape=(...  1.9 us
    ppermute x3, starting transfers between devices, shards(): lax.ppermute(sent[o - 1], ('col', 'sub'), [(i, (i + o) % lanes) for i in...  1.55 us
  transfers between devices with their start and end apart: 3, of which 2 were waited for; matrix products, arithmetic and copies ran while one was open for 0% of the time, Pallas kernels for 15%

profile of v4, /device:TPU:9, one launch (start us, length us, event | category | flops | bytes accessed | tf_op | source)
XLA Modules:
  0.0 49.5 jit_solution(7144114826921005147)
XLA Ops:
  0.6 0.0 copy-start.2
  0.6 0.0 copy-start.3
  0.7 0.0 copy-start.4
  0.7 0.0 copy-start
  0.7 0.0 copy-start.1
  0.7 2.4 %tables.1.tbl = s32[272]{0:T(512)} custom-call(s32[128]{0:T(128)} %pb_ref.1, s32[128]{0:T(128)} %pa_ref.1, s32[128]{0:T(128)} %wet_ref.1), custom_call_target="tpu_custom_call" | custom-call | flops 4000000000 | bytes 16777216 | tf_op jit(solution)/shard_map/tables/pallas_call | solution.py:470
  3.1 0.0 copy-done.2
  3.1 0.0 copy-done.3
  3.2 0.0 copy-done.4
  3.2 0.0 copy-done
  3.2 0.0 copy-done.1
  3.2 17.0 %halo.1 = (f32[4,4,128,128]{3,2,1,0:T(8,128)S(1)}, f32[4,8,32,128]{3,2,1,0:T(8,128)S(1)}, f32[4,8,32,128]{3,2,1,0:T(8,128)S(1)}) custom-call(f32[8,128,128]{2,1,0:T(8,128)S(1)} %copy-done, f32[8,128,128]{2,1,0:T(8,128)S(1)} %copy-done.1, f32[8,128,128]{2,1,0:T(8,128)S(1)} %copy-done.2, f32[8,128,128]{2,1,0:T(8,128)S(1)} %copy-done.3, ...), custom_call_target="tpu_custom_call" | custom-call | tf_op jit(solution)/shard_map/halo/pallas_call | solution.py:486
  20.2 0.0 copy-start.5
  20.2 0.7 %copy-done.5 = s32[272]{0:T(512)S(1)} copy-done((s32[272]{0:T(512)S(1)}, s32[272]{0:T(512)}, u32[]{:S(2)}) %copy-start.5) | copy-done | bytes 1112
  20.9 7.4 %steps.3 = (f32[3,2,128,128]{3,2,1,0:T(8,128)S(1)}, f32[3,2,128,128]{3,2,1,0:T(8,128)S(1)}, f32[3,2,128,128]{3,2,1,0:T(8,128)S(1)}) custom-call(s32[272]{0:T(512)S(1)} %copy-done.5, f32[8,128,128]{2,1,0:T(8,128)S(1)} %copy-done, f32[8,128,128]{2,1,0:T(8,128)S(1)} %copy-done.1, f32[8,128,128]{2,1,0:T(8,128)S(1)} %copy-done.2, f32[8,128,128]{2,1,0:T(8,128)S(1)} %copy-done.3, ...), custom_call_target="tpu_custom_call" | custom-call | flops 157286400 | bytes 8388608 | tf_op jit(solution)/shard_map/steps/pallas_call | solution.py:510
  28.2 0.3 collective-permute-start
  28.6 1.2 %collective-permute-start.1 = (f32[3,2,128,128]{3,2,1,0:T(8,128)S(1)}, f32[3,2,128,128]{3,2,1,0:T(8,128)S(1)}, u32[]{:S(2)}, u32[]{:S(2)}) collective-permute-start(f32[3,2,128,128]{3,2,1,0:T(8,128)S(1)} %get-tuple-element.13), channel_id=1, source_target_pairs={{0,2},{1,3},{2,0},{3,1},{4,6},{5,7},{6,4},{7,5},{8,10},{9,11},{10,... | collective-permute-start | bytes 1179656 | tf_op jit(solution)/shard_map/ppermute | solution.py:529
  29.8 0.0 collective-permute-start.2
  29.8 7.3 %steps.2.stay = f32[3,4,128,128]{3,2,1,0:T(8,128)S(1)} custom-call(s32[272]{0:T(512)S(1)} %copy-done.5, f32[8,128,128]{2,1,0:T(8,128)S(1)} %copy-done, f32[8,128,128]{2,1,0:T(8,128)S(1)} %copy-done.1, f32[8,128,128]{2,1,0:T(8,128)S(1)} %copy-done.2, f32[8,128,128]{2,1,0:T(8,128)S(1)} %copy-done.3, f32[8,128,128]{2,1,0:T(8,128)S(1)} %copy-done.4, ...), custom_call_target="tpu_custom_call" | custom-call | flops 157286400 | bytes 8388608 | tf_op jit(solution)/shard_map/steps/pallas_call | solution.py:510
  37.1 0.0 collective-permute-done.rest_0_
  37.1 9.5 %collective-permute-done.1.rest_1_ = f32[3,2,128,128]{3,2,1,0:T(8,128)S(1)} collective-permute-done((f32[3,2,128,128]{3,2,1,0:T(8,128)S(1)}, f32[3,2,128,128]{3,2,1,0:T(8,128)S(1)}, u32[]{:S(2)}, u32[]{:S(2)}) %collective-permute-start.1) | collective-permute-done | bytes 393248 | tf_op jit(solution)/shard_map/ppermute | solution.py:529
  46.7 0.9 %collective-permute-done.2.rest_2_ = f32[3,2,128,128]{3,2,1,0:T(8,128)S(1)} collective-permute-done((f32[3,2,128,128]{3,2,1,0:T(8,128)S(1)}, f32[3,2,128,128]{3,2,1,0:T(8,128)S(1)}, u32[]{:S(2)}, u32[]{:S(2)}) %collective-permute-start.2) | collective-permute-done | bytes 393248 | tf_op jit(solution)/shard_map/ppermute | solution.py:529
  47.6 1.9 %final.1 = (f32[8,128,128]{2,1,0:T(8,128)}, f32[8,128,128]{2,1,0:T(8,128)}, f32[8,128,128]{2,1,0:T(8,128)}) custom-call(s32[272]{0:T(512)S(1)} %copy-done.5, f32[3,4,128,128]{3,2,1,0:T(8,128)S(1)} %steps.2.stay, f32[3,2,128,128]{3,2,1,0:T(8,128)S(1)} %collective-permute-done.rest_0_, f32[3,2,128,128]{3,2,1,0:T(8,128)S(1)} %collective-permute-done.1.rest_1_, ...), custom_call_target="tpu_custom_call" | custom-call | tf_op jit(solution)/shard_map/final/pallas_call | solution.py:533
Async XLA Ops:
  0.6 2.5 %copy-start.2 = (f32[8,128,128]{2,1,0:T(8,128)S(1)}, f32[8,128,128]{2,1,0:T(8,128)}, u32[]{:S(2)}) copy-start(f32[8,128,128]{2,1,0:T(8,128)} %y.3) | copy-start | bytes 1572868
  0.6 2.5 %copy-start.3 = (f32[8,128,128]{2,1,0:T(8,128)S(1)}, f32[8,128,128]{2,1,0:T(8,128)}, u32[]{:S(2)}) copy-start(f32[8,128,128]{2,1,0:T(8,128)} %z.3) | copy-start | bytes 1572868
  0.7 2.5 %copy-start.4 = (f32[8,128,128]{2,1,0:T(8,128)S(1)}, f32[8,128,128]{2,1,0:T(8,128)}, u32[]{:S(2)}) copy-start(f32[8,128,128]{2,1,0:T(8,128)} %m.3) | copy-start | bytes 1572868
  0.7 2.5 %copy-start = (f32[8,128,128]{2,1,0:T(8,128)S(1)}, f32[8,128,128]{2,1,0:T(8,128)}, u32[]{:S(2)}) copy-start(f32[8,128,128]{2,1,0:T(8,128)} %h.3) | copy-start | bytes 1572868
  0.7 2.5 %copy-start.1 = (f32[8,128,128]{2,1,0:T(8,128)S(1)}, f32[8,128,128]{2,1,0:T(8,128)}, u32[]{:S(2)}) copy-start(f32[8,128,128]{2,1,0:T(8,128)} %x.3) | copy-start | bytes 1572868
  20.2 0.7 %copy-start.5 = (s32[272]{0:T(512)S(1)}, s32[272]{0:T(512)}, u32[]{:S(2)}) copy-start(s32[272]{0:T(512)} %tables.1.tbl) | copy-start | bytes 3268
  28.2 8.9 %collective-permute-start = (f32[3,2,128,128]{3,2,1,0:T(8,128)S(1)}, f32[3,2,128,128]{3,2,1,0:T(8,128)S(1)}, u32[]{:S(2)}, u32[]{:S(2)}) collective-permute-start(f32[3,2,128,128]{3,2,1,0:T(8,128)S(1)} %get-tuple-element.12), channel_id=1, source_target_pairs={{0,1},{1,2},{2,3},{3,0},{4,5},{5,6},{6,7},{7,4},{8,9},{9,10},{10,1... | collective-permute-start | bytes 1179656 | tf_op jit(solution)/shard_map/ppermute | solution.py:529
  28.6 18.1 %collective-permute-start.1 = (f32[3,2,128,128]{3,2,1,0:T(8,128)S(1)}, f32[3,2,128,128]{3,2,1,0:T(8,128)S(1)}, u32[]{:S(2)}, u32[]{:S(2)}) collective-permute-start(f32[3,2,128,128]{3,2,1,0:T(8,128)S(1)} %get-tuple-element.13), channel_id=1, source_target_pairs={{0,2},{1,3},{2,0},{3,1},{4,6},{5,7},{6,4},{7,5},{8,10},{9,11},{10,... | collective-permute-start | bytes 1179656 | tf_op jit(solution)/shard_map/ppermute | solution.py:529
  29.8 17.8 %collective-permute-start.2 = (f32[3,2,128,128]{3,2,1,0:T(8,128)S(1)}, f32[3,2,128,128]{3,2,1,0:T(8,128)S(1)}, u32[]{:S(2)}, u32[]{:S(2)}) collective-permute-start(f32[3,2,128,128]{3,2,1,0:T(8,128)S(1)} %get-tuple-element.14), channel_id=1, source_target_pairs={{0,3},{1,0},{2,1},{3,2},{4,7},{5,4},{6,5},{7,6},{8,11},{9,8},{10,9... | collective-permute-start | bytes 1179656 | tf_op jit(solution)/shard_map/ppermute | solution.py:529
